TPU v7x, 1024 devices: a whole 8x8x8 slice. The times are simulated.
1024 devices in a mesh: axial: 64 (over x, z), azim: 16 (over y, core).
Axes of the slice: x: 8, y: 8, z: 8, core: 2. Of those that a mesh axis runs over, the one named last changes fastest.
Arguments:
- gas_fields: float32 [3, 1024, 128, 128], P(None, 'axial', 'azim'), may hold values from -4 to 4
- drop_mass: float32 [2097152], P(('axial', 'azim')), may hold values from 0.2 to 2
- drop_temp: float32 [2097152], P(('axial', 'azim')), may hold values from -4 to 4
- drop_speed: float32 [2097152], P(('axial', 'azim')), may hold values from -4 to 4
- dest_first: int32 [2097152, 1], P(('axial', 'azim')), may hold values from 0 to 15; in each aligned block of 2048 rows (0 to 2047, 2048 to 4095, ...) at most 256 rows name the same one
- cell_first: int32 [2097152], P(('axial', 'azim')), may hold values from 0 to 16383
- dest_second: int32 [4194304, 1], P(('axial', 'azim')), may hold values from 0 to 15; in each aligned block of 4096 rows (0 to 4095, 4096 to 8191, ...) at most 256 rows name the same one
- cell_second: int32 [4194304], P(('axial', 'azim')), may hold values from 0 to 16383
Outputs:
- gas_next: float32 [3, 1024, 128, 128], P(None, 'axial', 'azim')
- drop_records: float32 [6, 4194304], P(None, ('axial', 'azim'))
Inputs may be any that keep to these rules, and one draw needn't show every extreme that they name: `dest_first`: in the rows of one device (aligned blocks of 2048 rows) no sector is named by more than 256 rows. `dest_second`: in the rows of one device (aligned blocks of 4096 rows) no sector is named by more than 256 rows. `cell_first`: local cell index (z * 8 + a) * 128 + r within the block of the device that holds the row. `cell_second`: local cell index (z * 8 + a) * 128 + r within the block of the device that holds the slot.
All inputs are finite; a program needn't handle non-finite values.
Results may differ from a plain program's by a relative error of at most 0.0003.
Values sent between devices are 32-bit elements; how exact they have to be, the bound alone decides.
No kernel may reach another device: no remote copies, remote signals or barrier semaphores. Data moves between devices by JAX's collectives and lax.ppermute only.
A program may use at most 32 MiB of HBM per device.

v0:
```python
import math

import jax
import jax.numpy as jnp
from jax import lax
from jax.sharding import PartitionSpec as P

DT_STEP = 0.01
TAU_HEAT = 0.04
TAU_MASS = 0.05
TAU_DRAG = 0.03
LATENT = 0.5
COUPLING = 1.0
FORCING = 4.0
ADVECT = 0.16
RADIUS_FLOOR = 0.7
DIFFUSION = (0.2, 0.15, 0.17)
WALL_VALUES = (1.0, 0.0, 0.0)


def padded_2(cells, sides, width):
    for axis, dim in sides:
        count = lax.axis_size(axis)
        head = lax.slice_in_dim(cells, 0, width, axis=dim)
        tail = lax.slice_in_dim(cells, cells.shape[dim] - width, cells.shape[dim], axis=dim)
        cells = jnp.concatenate(
            [
                lax.ppermute(tail, axis, [(i, (i + 1) % count) for i in range(count)]),
                cells,
                lax.ppermute(head, axis, [((i + 1) % count, i) for i in range(count)]),
            ],
            axis=dim,
        )
    return cells


def from_partner(value, axis, apart):
    mask = 2**apart
    pairs = [(source, source ^ mask) for source in range(lax.axis_size(axis))]
    return lax.ppermute(value, axis, pairs)


def increment(fields, z_next, z_prev, a_next, a_prev, opposite, sources, aspect):
    radial_count = fields.shape[3]
    wall_all = jnp.asarray(WALL_VALUES, jnp.float32).reshape(3, 1, 1, 1)
    radial_pad = jnp.concatenate(
        [
            opposite[..., 1:2],
            opposite[..., 0:1],
            fields,
            2.0 * wall_all - fields[..., -1:],
            2.0 * wall_all - fields[..., -2:-1],
        ],
        axis=3,
    )
    minus_two = radial_pad[..., 0:radial_count]
    minus_one = radial_pad[..., 1 : radial_count + 1]
    plus_one = radial_pad[..., 3 : radial_count + 3]
    plus_two = radial_pad[..., 4 : radial_count + 4]
    radial_pos = jnp.arange(radial_count, dtype=jnp.float32) + 0.5
    inverse = 1.0 / (12.0 * radial_pos)
    geometry = aspect * aspect / jnp.maximum(radial_pos / radial_count, RADIUS_FLOOR) ** 2
    laplace = (-plus_two + 16.0 * plus_one - 30.0 * fields + 16.0 * minus_one - minus_two) / 12.0
    laplace = laplace + (-plus_two + 8.0 * plus_one - 8.0 * minus_one + minus_two) * inverse
    laplace = laplace + geometry * (a_next + a_prev - 2.0 * fields)
    laplace = laplace + (z_next + z_prev - 2.0 * fields) / 16.0
    kappa_all = jnp.asarray(DIFFUSION, jnp.float32).reshape(3, 1, 1, 1)
    forcing_all = jnp.asarray((0.0, 0.0, FORCING), jnp.float32).reshape(3, 1, 1, 1)
    return (
        kappa_all * laplace
        - ADVECT * fields[2:3] * (z_next - z_prev)
        + DT_STEP * (sources + forcing_all)
    )


def droplet_terms(flat_gas, states, live_flag, cells):
    sample_gas = jnp.take(flat_gas, cells, axis=1)
    drop_mass = states[0]
    excess = 0.3 + 0.2 * jnp.tanh(states[1]) - sample_gas[1]
    evaporate = drop_mass * excess / TAU_MASS
    heating = sample_gas[0] - states[1]
    drag_diff = sample_gas[2] - states[2]
    change = (
        jnp.stack(
            [-evaporate, heating / TAU_HEAT - LATENT * excess / TAU_MASS, drag_diff / TAU_DRAG]
        )
        * live_flag
    )
    source_terms = jnp.stack(
        [
            -COUPLING * drop_mass * heating / TAU_HEAT,
            COUPLING * evaporate,
            -COUPLING * drop_mass * drag_diff / TAU_DRAG,
        ]
    )
    deposit = jnp.zeros_like(flat_gas).at[:, cells].add(source_terms)
    return (change, deposit)


def slot_ranks(targets, sectors):
    matches = (targets[:, None] == jnp.arange(sectors, dtype=jnp.int32)[None, :]).astype(jnp.int32)
    running = jnp.cumsum(matches, axis=0) - 1
    return jnp.sum(running * matches, axis=1)


def tendency(fields, sources, aspect):
    padded = padded_2(fields, (("axial", 1), ("azim", 2)), 1)
    across_bit = lax.axis_size("azim").bit_length() - 2
    opposite = from_partner(fields[:, :, :, :2], "azim", across_bit)
    return increment(
        fields,
        padded[:, 2:, 1:-1],
        padded[:, :-2, 1:-1],
        padded[:, 1:-1, 2:],
        padded[:, 1:-1, :-2],
        opposite,
        sources,
        aspect,
    )


def migrate(records, targets, capacity):
    sectors = lax.axis_size("azim")
    components = records.shape[0]
    target_list = targets[:, 0]
    position = target_list * capacity + slot_ranks(target_list, sectors)
    outgoing = jnp.zeros((components, sectors * capacity), jnp.float32).at[:, position].set(records)
    outgoing = outgoing.reshape(components, sectors, capacity)
    arrived = lax.all_to_all(outgoing, "azim", split_axis=1, concat_axis=1, tiled=True)
    return arrived.reshape(components, sectors * capacity)


def body(
    gas_fields, drop_mass, drop_temp, drop_speed, dest_first, cell_first, dest_second, cell_second
):
    sectors = lax.axis_size("azim")
    aspect = gas_fields.shape[2] * sectors / (2.0 * math.pi * gas_fields.shape[3])
    cap_first = 2 * drop_mass.shape[0] // sectors
    state_start = jnp.stack([drop_mass, drop_temp, drop_speed])
    live_start = (drop_mass > 0).astype(jnp.float32)
    change_first, deposit_first = droplet_terms(
        gas_fields.reshape(3, -1), state_start, live_start, cell_first
    )
    gas_middle = gas_fields + tendency(gas_fields, deposit_first.reshape(gas_fields.shape), aspect)
    state_middle = state_start + DT_STEP * change_first
    moved = migrate(jnp.concatenate([state_middle, state_start], axis=0), dest_first, cap_first)
    state_now = moved[:3]
    state_anchor = moved[3:]
    live_now = (state_anchor[0] > 0).astype(jnp.float32)
    change_second, deposit_second = droplet_terms(
        gas_middle.reshape(3, -1), state_now, live_now, cell_second
    )
    gas_next = 0.75 * gas_fields + 0.25 * (
        gas_middle + tendency(gas_middle, deposit_second.reshape(gas_fields.shape), aspect)
    )
    state_final = 0.75 * state_anchor + 0.25 * (state_now + DT_STEP * change_second)
    drop_records = migrate(
        jnp.concatenate([state_final, state_anchor], axis=0), dest_second, cap_first
    )
    return (gas_next, drop_records)


def solution(mesh):
    placed = (
        P(None, "axial", "azim", None),
        P(("axial", "azim")),
        P(("axial", "azim")),
        P(("axial", "azim")),
        P(("axial", "azim"), None),
        P(("axial", "azim")),
        P(("axial", "azim"), None),
        P(("axial", "azim")),
    )
    return jax.shard_map(
        body,
        mesh=mesh,
        in_specs=placed,
        out_specs=(P(None, "axial", "azim", None), P(None, ("axial", "azim"))),
        check_vma=False,
    )
```

profile of v0, /device:TPU:1, one launch (start us, length us, event | category | flops | bytes accessed | tf_op | source)
XLA Modules:
  0.0 200.4 jit_solution(3887908101292280093)
XLA Ops:
  0.6 1.3 fusion.48
  2.0 5.7 %collective-permute-start.1 = (f32[3,1,8,128]{3,2,1,0:T(8,128)}, f32[3,1,8,128]{3,2,1,0:T(8,128)}, u32[]{:S(2)}, u32[]{:S(2)}) collective-permute-start(f32[3,1,8,128]{3,2,1,0:T(8,128)} %get-tuple-element.25), channel_id=1, source_target_pairs={{0,16},{16,32},{32,48},{48,64},{64,80},{80,96},{96,112},{112,128},... | collective-permute-start | bytes 36872 | tf_op jit(solution)/shard_map/ppermute | solution.py:28
  7.7 16.4 %collective-permute-start.2 = (f32[3,1,8,128]{3,2,1,0:T(8,128)}, f32[3,1,8,128]{3,2,1,0:T(8,128)}, u32[]{:S(2)}, u32[]{:S(2)}) collective-permute-start(f32[3,1,8,128]{3,2,1,0:T(8,128)} %get-tuple-element.24), channel_id=1, source_target_pairs={{16,0},{32,16},{48,32},{64,48},{80,64},{96,80},{112,96},{128,112},... | collective-permute-start | bytes 36872 | tf_op jit(solution)/shard_map/ppermute | solution.py:30
  24.1 7.9 %collective-permute-start = (f32[3,16,8,2]{3,2,1,0:T(8,128)}, f32[3,16,8,2]{3,2,1,0:T(8,128)S(1)}, u32[]{:S(2)}, u32[]{:S(2)}) collective-permute-start(f32[3,16,8,2]{3,2,1,0:T(8,128)} %bitcast.82), channel_id=1, source_target_pairs={{0,8},{1,9},{2,10},{3,11},{4,12},{5,13},{6,14},{7,15},{8,0},{9,1},... | collective-permute-start | bytes 9224 | tf_op jit(solution)/shard_map/ppermute | solution.py:40
  32.0 5.6 %copy.69 = f32[3,16,8,128]{0,3,2,1:T(8,128)} copy(f32[3,16,8,128]{3,2,1,0:T(8,128)} %param.14) | data formatting | bytes 393216 | tf_op args[0]
  38.2 8.8 %gather_fusion = f32[2048,3]{1,0:T(8,128)S(1)} fusion(f32[3,16384]{0,1:T(8,128)} %bitcast.79, s32[2048]{0:T(1024)S(1)} %get-tuple-element.48), kind=kCustom, calls=%fused_computation | custom fusion | bytes 57344 | tf_op jit(solution)/shard_map/jit(_take)/gather | solution.py:77
  47.4 1.4 slice_reduce_fusion.2
  50.0 4.5 %reduce-window.14 = s32[16,16,128]{2,1,0:T(8,128)S(1)} reduce-window(s32[16,16,128]{2,1,0:T(8,128)S(1)} %fusion.35, s32[]{:T(128)} %constant.57.clone.1), window={size=1x1x128 pad=0_0x0_0x127_0}, to_apply=%region_1.2 | reduce-window | flops 4161536 | bytes 262148 | tf_op jit(solution)/shard_map/reduce-window
  56.0 6.2 %scatter_custom_fusion.1 = f32[6,4096]{0,1:T(8,128)S(1)} fusion(s32[2048]{0:T(1024)} %bitcast.116, f32[2048,6]{1,0:T(8,128)S(1)} %copy.72, f32[]{:T(128)} %constant.56.clone.1), kind=kCustom, calls=%fused_computation.16 | custom fusion | bytes 98816 | tf_op jit(solution)/shard_map/scatter | solution.py:127
  62.2 1.3 copy.73
  63.5 4.7 %all-to-all-start = ((f32[6,16,256]{2,0,1:T(8,128)}), f32[6,16,256]{2,0,1:T(8,128)S(1)}, u32[]{:S(2)}, u32[]{:S(2)}) async-start(f32[6,16,256]{2,0,1:T(8,128)} %copy.73), calls=%async_computation | async-start | bytes 262144 | tf_op jit(solution)/shard_map/all_to_all | solution.py:129
  69.6 4.6 %reduce-window.16 = s32[16,32,128]{2,1,0:T(8,128)S(1)} reduce-window(s32[16,32,128]{2,1,0:T(8,128)S(1)} %fusion.10, s32[]{:T(128)} %constant.57.clone.1), window={size=1x1x128 pad=0_0x0_0x127_0}, to_apply=%region_6.7 | reduce-window | flops 8323072 | bytes 524292 | tf_op jit(solution)/shard_map/reduce-window.2
  76.3 15.3 %scatter_custom_fusion = f32[3,16384]{0,1:T(8,128)} fusion(s32[2048]{0:T(1024)} %get-tuple-element.49, f32[2048,3]{1,0:T(8,128)S(1)} %copy.70, f32[]{:T(128)} %constant.56.clone.1), kind=kCustom, calls=%fused_computation.8 | custom fusion | flops 6144 | bytes 197120 | tf_op jit(solution)/shard_map/scatter-add | solution.py:96
  91.6 5.2 %copy.71 = f32[3,16,8,128]{3,2,1,0:T(8,128)S(1)} copy(f32[3,16,8,128]{0,3,2,1:T(8,128)} %bitcast.77) | data formatting | bytes 393216 | tf_op jit(solution)/shard_map/reshape | solution.py:144
  96.9 0.7 constant_dynamic-update-slice_fusion.2
  98.6 1.5 collective-permute-start.4
  100.3 1.4 collective-permute-done.3
  102.2 1.2 fusion.31
  103.4 4.6 %copy.74 = f32[3,16,8,128]{0,3,2,1:T(8,128)} copy(f32[3,16,8,128]{3,2,1,0:T(8,128)S(1)} %fusion.31) | data formatting | bytes 393216 | tf_op jit(solution)/shard_map/add | solution.py:144
  108.3 14.1 %gather_fusion.1 = f32[4096,3]{1,0:T(8,128)S(1)} fusion(f32[3,16384]{0,1:T(8,128)} %bitcast.78, s32[4096]{0:T(1024)S(1)} %get-tuple-element.38), kind=kCustom, calls=%fused_computation.1 | custom fusion | bytes 114688 | tf_op jit(solution)/shard_map/jit(_take)/gather | solution.py:77
  123.0 6.8 %collective-permute-start.5 = (f32[3,16,8,2]{3,2,1,0:T(8,128)S(1)}, f32[3,16,8,2]{3,2,1,0:T(8,128)S(1)}, u32[]{:S(2)}, u32[]{:S(2)}) collective-permute-start(f32[3,16,8,2]{3,2,1,0:T(8,128)S(1)} %bitcast.83), channel_id=1, source_target_pairs={{0,8},{1,9},{2,10},{3,11},{4,12},{5,13},{6,14},{7,15},{8,0},{9,1},... | collective-permute-start | bytes 9224 | tf_op jit(solution)/shard_map/ppermute | solution.py:40
  129.9 1.9 collective-permute-start.6
  131.8 6.9 %collective-permute-start.7 = (f32[3,1,8,128]{3,2,1,0:T(8,128)S(1)}, f32[3,1,8,128]{3,2,1,0:T(8,128)S(1)}, u32[]{:S(2)}, u32[]{:S(2)}) collective-permute-start(f32[3,1,8,128]{3,2,1,0:T(8,128)S(1)} %get-tuple-element.21), channel_id=1, source_target_pairs={{16,0},{32,16},{48,32},{64,48},{80,64},{96,80},{112,96},{128,112},... | collective-permute-start | bytes 36872 | tf_op jit(solution)/shard_map/ppermute | solution.py:30
  139.9 3.3 %collective-permute-start.8 = (f32[3,18,1,128]{3,2,1,0:T(1,128)}, f32[3,18,1,128]{3,2,1,0:T(1,128)}, u32[]{:S(2)}, u32[]{:S(2)}) collective-permute-start(f32[3,18,1,128]{3,2,1,0:T(1,128)} %get-tuple-element.10), channel_id=1, source_target_pairs={{1,0},{2,1},{3,2},{4,3},{5,4},{6,5},{7,6},{8,7},{9,8},{10,9},{11,1... | collective-permute-start | bytes 82952 | tf_op jit(solution)/shard_map/ppermute | solution.py:30
  144.2 2.0 copy.78
  146.2 11.4 %scatter_custom_fusion.3 = f32[6,4096]{0,1:T(8,128)S(1)} fusion(s32[4096]{0:T(1024)} %bitcast.115, f32[4096,6]{1,0:T(8,128)} %copy.78, f32[]{:T(128)} %constant.56.clone.1), kind=kCustom, calls=%fused_computation.14 | custom fusion | bytes 98816 | tf_op jit(solution)/shard_map/scatter | solution.py:127
  157.6 1.3 copy.79
  158.9 5.9 %all-to-all-start.1 = ((f32[6,16,256]{2,0,1:T(8,128)}), f32[6,16,256]{2,0,1:T(8,128)S(1)}, u32[]{:S(2)}, u32[]{:S(2)}) async-start(f32[6,16,256]{2,0,1:T(8,128)} %copy.79), calls=%async_computation.1 | async-start | bytes 262144 | tf_op jit(solution)/shard_map/all_to_all | solution.py:129
  164.8 0.8 maximum_bitcast_fusion.2
  166.3 26.2 %scatter_custom_fusion.2 = f32[3,16384]{0,1:T(8,128)} fusion(s32[4096]{0:T(1024)} %get-tuple-element.39, f32[4096,3]{1,0:T(8,128)S(1)} %copy.76, f32[]{:T(128)} %constant.56.clone.1), kind=kCustom, calls=%fused_computation.6 | custom fusion | flops 12288 | bytes 197120 | tf_op jit(solution)/shard_map/scatter-add | solution.py:96
  192.5 5.3 %copy.77 = f32[3,16,8,128]{3,2,1,0:T(8,128)S(1)} copy(f32[3,16,8,128]{0,3,2,1:T(8,128)} %bitcast.76) | data formatting | bytes 393216 | tf_op jit(solution)/shard_map/reshape | solution.py:154
  197.8 1.9 fusion.21
  (112 shorter events, 12.8 us)
Async XLA Ops:
  2.0 94.9 %collective-permute-start.1 = (f32[3,1,8,128]{3,2,1,0:T(8,128)}, f32[3,1,8,128]{3,2,1,0:T(8,128)}, u32[]{:S(2)}, u32[]{:S(2)}) collective-permute-start(f32[3,1,8,128]{3,2,1,0:T(8,128)} %get-tuple-element.25), channel_id=1, source_target_pairs={{0,16},{16,32},{32,48},{48,64},{64,80},{80,96},{96,112},{112,128},... | collective-permute-start | bytes 36872 | tf_op jit(solution)/shard_map/ppermute | solution.py:28
  7.7 89.9 %collective-permute-start.2 = (f32[3,1,8,128]{3,2,1,0:T(8,128)}, f32[3,1,8,128]{3,2,1,0:T(8,128)}, u32[]{:S(2)}, u32[]{:S(2)}) collective-permute-start(f32[3,1,8,128]{3,2,1,0:T(8,128)} %get-tuple-element.24), channel_id=1, source_target_pairs={{16,0},{32,16},{48,32},{64,48},{80,64},{96,80},{112,96},{128,112},... | collective-permute-start | bytes 36872 | tf_op jit(solution)/shard_map/ppermute | solution.py:30
  24.1 13.5 %copy-start.11 = (s32[2048]{0:T(1024)S(1)}, s32[2048]{0:T(1024)}, u32[]{:S(2)}) copy-start(s32[2048]{0:T(1024)} %param.19) | copy-start | bytes 24580
  24.1 76.1 %collective-permute-start = (f32[3,16,8,2]{3,2,1,0:T(8,128)}, f32[3,16,8,2]{3,2,1,0:T(8,128)S(1)}, u32[]{:S(2)}, u32[]{:S(2)}) collective-permute-start(f32[3,16,8,2]{3,2,1,0:T(8,128)} %bitcast.82), channel_id=1, source_target_pairs={{0,8},{1,9},{2,10},{3,11},{4,12},{5,13},{6,14},{7,15},{8,0},{9,1},... | collective-permute-start | bytes 9224 | tf_op jit(solution)/shard_map/ppermute | solution.py:40
  56.0 12.2 %copy-start = (f32[3,16,8,128]{3,2,1,0:T(8,128)S(1)}, f32[3,16,8,128]{3,2,1,0:T(8,128)}, u32[]{:S(2)}) copy-start(f32[3,16,8,128]{3,2,1,0:T(8,128)} %param.14) | copy-start | bytes 589828
  56.0 12.2 %copy-start.6 = (s32[4096]{0:T(1024)S(1)}, s32[4096]{0:T(1024)}, u32[]{:S(2)}) copy-start(s32[4096]{0:T(1024)} %param.21) | copy-start | bytes 49156
  62.2 7.2 %copy-start.24 = (f32[3]{0:T(128)S(1)}, f32[3]{0:T(128)}, u32[]{:S(2)}) copy-start(f32[3]{0:T(128)} %constant.143) | copy-start | bytes 40
  62.2 7.4 %copy-start.1 = (s32[4096,1]{0,1:T(1,128)S(1)}, s32[4096,1]{0,1:T(1,128)}, u32[]{:S(2)}) copy-start(s32[4096,1]{0,1:T(1,128)} %param.20) | copy-start | bytes 49156
  63.5 12.4 %copy-start.12 = (f32[2048]{0:T(1024)S(1)}, f32[2048]{0:T(1024)}, u32[]{:S(2)}) copy-start(f32[2048]{0:T(1024)} %get-tuple-element.43) | copy-start | bytes 24580
  63.5 12.4 %copy-start.13 = (f32[2048]{0:T(1024)S(1)}, f32[2048]{0:T(1024)}, u32[]{:S(2)}) copy-start(f32[2048]{0:T(1024)} %get-tuple-element.44) | copy-start | bytes 24580
  63.5 12.4 %copy-start.14 = (f32[2048]{0:T(1024)S(1)}, f32[2048]{0:T(1024)}, u32[]{:S(2)}) copy-start(f32[2048]{0:T(1024)} %get-tuple-element.47) | copy-start | bytes 24580
  63.5 79.7 %all-to-all-start = ((f32[6,16,256]{2,0,1:T(8,128)}), f32[6,16,256]{2,0,1:T(8,128)S(1)}, u32[]{:S(2)}, u32[]{:S(2)}) async-start(f32[6,16,256]{2,0,1:T(8,128)} %copy.73), calls=%async_computation | async-start | bytes 262144 | tf_op jit(solution)/shard_map/all_to_all | solution.py:129
  75.9 26.2 %copy-start.20 = (f32[128]{0:T(128)}, f32[128]{0:T(128)S(1)}, u32[]{:S(2)}) copy-start(f32[128]{0:T(128)S(1)} %get-tuple-element.50) | copy-start | bytes 1540
  75.9 26.2 %copy-start.22 = (f32[128]{0:T(128)}, f32[128]{0:T(128)S(1)}, u32[]{:S(2)}) copy-start(f32[128]{0:T(128)S(1)} %get-tuple-element.51) | copy-start | bytes 1540
  91.6 10.5 %copy-start.16 = (f32[3]{0:T(128)S(1)}, f32[3]{0:T(128)}, u32[]{:S(2)}) copy-start(f32[3]{0:T(128)} %constant.140.clone) | copy-start | bytes 40
  91.6 10.6 %copy-start.18 = (f32[3]{0:T(128)S(1)}, f32[3]{0:T(128)}, u32[]{:S(2)}) copy-start(f32[3]{0:T(128)} %constant.141.clone) | copy-start | bytes 40
  98.4 3.3 %collective-permute-start.3 = (f32[3,18,1,128]{3,2,1,0:T(1,128)S(1)}, f32[3,18,1,128]{3,2,1,0:T(1,128)S(1)}, u32[]{:S(2)}, u32[]{:S(2)}) collective-permute-start(f32[3,18,1,128]{3,2,1,0:T(1,128)S(1)} %get-tuple-element.12), channel_id=1, source_target_pairs={{1,0},{2,1},{3,2},{4,3},{5,4},{6,5},{7,6},{8,7},{9,8},{10,9},{11,1... | collective-permute-start | bytes 82952 | tf_op jit(solution)/shard_map/ppermute | solution.py:30
  98.6 3.5 %collective-permute-start.4 = (f32[3,18,1,128]{3,2,1,0:T(1,128)S(1)}, f32[3,18,1,128]{3,2,1,0:T(1,128)S(1)}, u32[]{:S(2)}, u32[]{:S(2)}) collective-permute-start(f32[3,18,1,128]{3,2,1,0:T(1,128)S(1)} %get-tuple-element.13), channel_id=1, source_target_pairs={{0,1},{1,2},{2,3},{3,4},{4,5},{5,6},{6,7},{7,8},{8,9},{9,10},{10,1... | collective-permute-start | bytes 82952 | tf_op jit(solution)/shard_map/ppermute | solution.py:28
  103.4 4.6 %copy-start.25 = (f32[3]{0:T(128)S(1)}, f32[3]{0:T(128)}, u32[]{:S(2)}) copy-start(f32[3]{0:T(128)} %constant.143) | copy-start | bytes 40
  108.1 21.8 %copy-start.15 = (pred[4096]{0:T(1024)(128)(4,1)S(1)}, pred[4096]{0:T(1024)(128)(4,1)}, u32[]{:S(2)}) copy-start(pred[4096]{0:T(1024)(128)(4,1)} %compare_and_fusion) | copy-start | bytes 12292
  123.0 15.6 %collective-permute-start.5 = (f32[3,16,8,2]{3,2,1,0:T(8,128)S(1)}, f32[3,16,8,2]{3,2,1,0:T(8,128)S(1)}, u32[]{:S(2)}, u32[]{:S(2)}) collective-permute-start(f32[3,16,8,2]{3,2,1,0:T(8,128)S(1)} %bitcast.83), channel_id=1, source_target_pairs={{0,8},{1,9},{2,10},{3,11},{4,12},{5,13},{6,14},{7,15},{8,0},{9,1},... | collective-permute-start | bytes 9224 | tf_op jit(solution)/shard_map/ppermute | solution.py:40
  129.9 8.9 %collective-permute-start.6 = (f32[3,1,8,128]{3,2,1,0:T(8,128)S(1)}, f32[3,1,8,128]{3,2,1,0:T(8,128)S(1)}, u32[]{:S(2)}, u32[]{:S(2)}) collective-permute-start(f32[3,1,8,128]{3,2,1,0:T(8,128)S(1)} %get-tuple-element.20), channel_id=1, source_target_pairs={{0,16},{16,32},{32,48},{48,64},{64,80},{80,96},{96,112},{112,128},... | collective-permute-start | bytes 36872 | tf_op jit(solution)/shard_map/ppermute | solution.py:28
  131.8 7.5 %collective-permute-start.7 = (f32[3,1,8,128]{3,2,1,0:T(8,128)S(1)}, f32[3,1,8,128]{3,2,1,0:T(8,128)S(1)}, u32[]{:S(2)}, u32[]{:S(2)}) collective-permute-start(f32[3,1,8,128]{3,2,1,0:T(8,128)S(1)} %get-tuple-element.21), channel_id=1, source_target_pairs={{16,0},{32,16},{48,32},{64,48},{80,64},{96,80},{112,96},{128,112},... | collective-permute-start | bytes 36872 | tf_op jit(solution)/shard_map/ppermute | solution.py:30
  139.9 57.8 %collective-permute-start.8 = (f32[3,18,1,128]{3,2,1,0:T(1,128)}, f32[3,18,1,128]{3,2,1,0:T(1,128)}, u32[]{:S(2)}, u32[]{:S(2)}) collective-permute-start(f32[3,18,1,128]{3,2,1,0:T(1,128)} %get-tuple-element.10), channel_id=1, source_target_pairs={{1,0},{2,1},{3,2},{4,3},{5,4},{6,5},{7,6},{8,7},{9,8},{10,9},{11,1... | collective-permute-start | bytes 82952 | tf_op jit(solution)/shard_map/ppermute | solution.py:30
  143.2 54.5 %collective-permute-start.9 = (f32[3,18,1,128]{3,2,1,0:T(1,128)}, f32[3,18,1,128]{3,2,1,0:T(1,128)}, u32[]{:S(2)}, u32[]{:S(2)}) collective-permute-start(f32[3,18,1,128]{3,2,1,0:T(1,128)} %get-tuple-element.11), channel_id=1, source_target_pairs={{0,1},{1,2},{2,3},{3,4},{4,5},{5,6},{6,7},{7,8},{8,9},{9,10},{10,1... | collective-permute-start | bytes 82952 | tf_op jit(solution)/shard_map/ppermute | solution.py:28
  158.9 40.9 %all-to-all-start.1 = ((f32[6,16,256]{2,0,1:T(8,128)}), f32[6,16,256]{2,0,1:T(8,128)S(1)}, u32[]{:S(2)}, u32[]{:S(2)}) async-start(f32[6,16,256]{2,0,1:T(8,128)} %copy.79), calls=%async_computation.1 | async-start | bytes 262144 | tf_op jit(solution)/shard_map/all_to_all | solution.py:129
  192.4 5.3 %copy-start.8 = (f32[3,1,8,128]{3,2,1,0:T(8,128)S(1)}, f32[3,1,8,128]{3,2,1,0:T(8,128)}, u32[]{:S(2)}) copy-start(f32[3,1,8,128]{3,2,1,0:T(8,128)} %copy-done.7) | copy-start | bytes 36868
  192.5 5.3 %copy-start.10 = (f32[3,1,8,128]{3,2,1,0:T(8,128)S(1)}, f32[3,1,8,128]{3,2,1,0:T(8,128)}, u32[]{:S(2)}) copy-start(f32[3,1,8,128]{3,2,1,0:T(8,128)} %copy-done.9) | copy-start | bytes 36868
  192.5 5.3 %copy-start.17 = (f32[3]{0:T(128)S(1)}, f32[3]{0:T(128)}, u32[]{:S(2)}) copy-start(f32[3]{0:T(128)} %constant.140.clone) | copy-start | bytes 40
  192.5 5.3 %copy-start.19 = (f32[3]{0:T(128)S(1)}, f32[3]{0:T(128)}, u32[]{:S(2)}) copy-start(f32[3]{0:T(128)} %constant.141.clone) | copy-start | bytes 40
  192.5 5.3 %copy-start.21 = (f32[128]{0:T(128)S(1)}, f32[128]{0:T(128)}, u32[]{:S(2)}) copy-start(f32[128]{0:T(128)} %copy-done.20) | copy-start | bytes 1540
  192.5 5.3 %copy-start.23 = (f32[128]{0:T(128)S(1)}, f32[128]{0:T(128)}, u32[]{:S(2)}) copy-start(f32[128]{0:T(128)} %copy-done.22) | copy-start | bytes 1540
  (6 other events, 15.5 us)
where the time goes:
time: 202 us; the launch traced here: 200 us
  local copies, waits for them, and re-layouts  74 us (37%)
  other arithmetic  61.5 us (30%)
  starting transfers between devices  61.2 us (30%)
  waiting for transfers between devices  2.41 us (1%)
    scatter-add x2, other arithmetic, droplet_terms(): deposit = jnp.zeros_like(flat_gas).at[:, cells].add(source_terms)  41.5 us
    ppermute x4, starting transfers between devices, padded_2(): lax.ppermute(head, axis, [((i + 1) % count, i) for i in range(count)])  26.7 us
    gather x3, local copies, waits for them, and re-layouts, droplet_terms(): sample_gas = jnp.take(flat_gas, cells, axis=1)  23.6 us
    scatter x2, local copies, waits for them, and re-layouts, migrate(): jnp.zeros((components, sectors * capacity), jnp.float32).at[:, position]  17.6 us
    ppermute x2, starting transfers between devices, from_partner(): return lax.ppermute(value, axis, pairs)  14.7 us
    all_to_all x2, starting transfers between devices, migrate(): lax.all_to_all(outgoing, 'azim', split_axis=1, concat_axis=1, tiled=True)  10.6 us
    another operation x4, other arithmetic  9.52 us
    ppermute x4, starting transfers between devices, padded_2(): lax.ppermute(tail, axis, [(i, (i + 1) % count) for i in range(count)])  9.17 us
  transfers between devices with their start and end apart: 12, of which 3 were waited for; matrix products, arithmetic and copies ran while one was open for 67% of the time, Pallas kernels for 0%

commit v1 on v0

v1 whole, which is shorter than its diff:
```python
import math

import jax
import jax.numpy as jnp
from jax import lax
from jax.experimental import pallas as pl
from jax.experimental.pallas import tpu as pltpu
from jax.sharding import PartitionSpec as P

DT_STEP = 0.01
TAU_HEAT = 0.04
TAU_MASS = 0.05
TAU_DRAG = 0.03
LATENT = 0.5
COUPLING = 1.0
FORCING = (0.0, 0.0, 4.0)
ADVECT = 0.16
RADIUS_FLOOR = 0.7
DIFFUSION = (0.2, 0.15, 0.17)
WALL_VALUES = (1.0, 0.0, 0.0)

F32 = jnp.float32
BF16 = jnp.bfloat16
LANES = 128
SUB = 8
VMEM_LIMIT = 40 << 20


def iota(shape, dim):
    return lax.broadcasted_iota(jnp.int32, shape, dim)


def one_hot(row, size):
    hit = iota((size, row.shape[1]), 0) == row
    return jnp.where(hit, 1.0, 0.0).astype(BF16)


def halves(x):
    head = x.astype(BF16)
    return head, (x - head.astype(F32)).astype(BF16)


def wide_row(ref, j):
    return jnp.concatenate([ref[pl.ds(j, 1), :], ref[pl.ds(j + 1, 1), :]], axis=1)


def dot_nt(a, b):
    return lax.dot_general(a, b, (((1,), (1,)), ((), ())), preferred_element_type=F32)


def gas_table(planes):
    turned = [p.T for p in planes]
    parts = [jnp.concatenate(halves(t), axis=1) for t in turned]
    return jnp.concatenate(parts, axis=0), turned


def sample(table, cell_ref, out_ref):
    size = table.shape[1] // 2
    lanes_r = table.shape[0] // 3
    shift = lanes_r.bit_length() - 1
    for j in range(0, cell_ref.shape[0], 2):
        cell = wide_row(cell_ref, j)
        pick = one_hot(cell >> shift, size)
        mixed = jnp.dot(table, jnp.concatenate([pick, pick], axis=0), preferred_element_type=F32)
        here = iota((lanes_r, cell.shape[1]), 0) == (cell & (lanes_r - 1))
        for c in range(3):
            part = jnp.where(here, mixed[c * lanes_r : (c + 1) * lanes_r], 0.0)
            row = jnp.sum(part, axis=0, keepdims=True)
            out_ref[c, pl.ds(j, 1), :] = row[:, :LANES]
            out_ref[c, pl.ds(j + 1, 1), :] = row[:, LANES:]


def droplet_rates(states, gas, live):
    mass, temp, speed = states
    excess = 0.3 + 0.2 * jnp.tanh(temp) - gas[1]
    evaporate = mass * excess / TAU_MASS
    heating = gas[0] - temp
    drag = gas[2] - speed
    change = (
        -evaporate * live,
        (heating / TAU_HEAT - LATENT * excess / TAU_MASS) * live,
        drag / TAU_DRAG * live,
    )
    source = (
        -COUPLING * mass * heating / TAU_HEAT,
        COUPLING * evaporate,
        -COUPLING * mass * drag / TAU_DRAG,
    )
    return change, source


def deposit(source_ref, cell_ref, rows, lanes_r):
    shift = lanes_r.bit_length() - 1
    total = None
    for j in range(0, cell_ref.shape[0], 2):
        cell = wide_row(cell_ref, j)
        pick = one_hot(cell >> shift, rows)
        here = iota((lanes_r, cell.shape[1]), 0) == (cell & (lanes_r - 1))
        spread = []
        for c in range(3):
            parts = halves(wide_row(source_ref.at[c], j))
            spread.append(
                jnp.concatenate(
                    [jnp.where(here, p.astype(F32), 0.0).astype(BF16) for p in parts], axis=1
                )
            )
        piece = dot_nt(jnp.concatenate([pick, pick], axis=1), jnp.concatenate(spread, axis=0))
        total = piece if total is None else total + piece
    return total


def slot_of(dest, sectors, capacity):
    n = dest.shape[0]
    hits = jnp.concatenate(
        [jnp.where(dest == t, 1.0, 0.0) for t in range(sectors)], axis=0
    ).astype(BF16)
    upto = jnp.where(iota((LANES, LANES), 0) <= iota((LANES, LANES), 1), 1.0, 0.0).astype(BF16)
    inside = jnp.dot(hits, upto, preferred_element_type=F32)
    every = jnp.dot(hits, jnp.ones((LANES, LANES), BF16), preferred_element_type=F32)
    before = jnp.where(iota((n, n), 1) < iota((n, n), 0), 1.0, 0.0).astype(BF16)
    rank = jnp.zeros(dest.shape, F32)
    for t in range(sectors):
        rows = slice(t * n, (t + 1) * n)
        carry = jnp.dot(before, every[rows].astype(BF16), preferred_element_type=F32)
        rank = rank + jnp.where(dest == t, inside[rows] + carry, 0.0)
    return dest * capacity + rank.astype(jnp.int32) - 1


def place(record_ref, slot_ref, blocks):
    total = None
    for j in range(0, slot_ref.shape[0], 2):
        slot = wide_row(slot_ref, j)
        lane = one_hot(slot & (LANES - 1), LANES)
        block = slot >> (LANES.bit_length() - 1)
        record = jnp.concatenate(
            [record_ref[pl.ds(SUB * j, SUB), :], record_ref[pl.ds(SUB * (j + 1), SUB), :]], axis=1
        )
        parts = [p.astype(F32) for p in halves(record)]
        spread = [
            jnp.concatenate(
                [jnp.where(block == b, p, 0.0) for b in range(blocks)], axis=0
            ).astype(BF16)
            for p in parts
        ]
        piece = dot_nt(jnp.concatenate(spread, axis=1), jnp.concatenate([lane, lane], axis=1))
        total = piece if total is None else total + piece
    return total


def send_records(out_ref, placed, turned):
    sectors = out_ref.shape[0]
    out_ref[:, : 2 * SUB, :] = placed.reshape(sectors, 2 * SUB, LANES)
    near = jnp.concatenate([t[:2] for t in turned] + [jnp.zeros((2, LANES), F32)], axis=0)
    for t in range(sectors):
        out_ref[t, 2 * SUB :, :] = near


def edges(planes_ref, first_z, last_z, first_a, last_a, count_z, count_a):
    for c in range(3):
        first_z[c] = planes_ref[c, :count_a, :]
        last_z[c] = planes_ref[c, (count_z - 1) * count_a :, :]
        first_a[c] = planes_ref[c, pl.ds(0, count_z, stride=count_a), :]
        last_a[c] = planes_ref[c, pl.ds(count_a - 1, count_z, stride=count_a), :]


def first_kernel(
    gas, mass, temp, speed, cell, dest, out, source, first_z, last_z, first_a, last_a, gathered, slots, records
):
    sectors = out.shape[0]
    count_a = first_z.shape[1]
    count_z = first_a.shape[1]
    table, turned = gas_table([gas[c] for c in range(3)])
    sample(table, cell, gathered)
    states = (mass[...], temp[...], speed[...])
    live = jnp.where(states[0] > 0, 1.0, 0.0)
    change, terms = droplet_rates(states, [gathered[c] for c in range(3)], live)
    n = cell.shape[0]
    records[...] = jnp.zeros(records.shape, F32)
    for c in range(3):
        source[c] = terms[c]
        records[pl.ds(c, n, stride=SUB), :] = states[c] + DT_STEP * change[c]
        records[pl.ds(3 + c, n, stride=SUB), :] = states[c]
    slots[...] = slot_of(dest[...], sectors, 2 * LANES)
    send_records(out, place(records, slots, 2 * sectors), turned)
    edges(gas, first_z, last_z, first_a, last_a, count_z, count_a)


def deposit_kernel(source, cell, out):
    total = deposit(source, cell, out.shape[1], out.shape[2])
    for c in range(3):
        out[c] = total[:, c * LANES : (c + 1) * LANES]


def stencil(gas, added, z_next, z_prev, a_next, a_prev, near, aspect, count_z, count_a):
    shape = (count_z, count_a, LANES)
    radius = iota((1, 1, LANES), 2)
    pos = radius.astype(F32) + 0.5
    inverse = 1.0 / (12.0 * pos)
    geometry = aspect * aspect / jnp.maximum(pos / LANES, RADIUS_FLOOR) ** 2
    across = jnp.concatenate([near, jnp.zeros((LANES - SUB, LANES), F32)], axis=0).T
    lane = iota(shape, 2)
    column = iota(shape, 1)
    fields = [gas[c].reshape(shape) for c in range(3)]
    results = []
    for c in range(3):
        q = fields[c]
        edge = 2.0 * WALL_VALUES[c]
        near_0 = across[:, 2 * c : 2 * c + 1].reshape(count_z, count_a, 1)
        near_1 = across[:, 2 * c + 1 : 2 * c + 2].reshape(count_z, count_a, 1)
        up = pltpu.roll(q, LANES - 1, 2)
        down = pltpu.roll(q, 1, 2)
        up_2 = pltpu.roll(q, LANES - 2, 2)
        down_2 = pltpu.roll(q, 2, 2)
        plus_one = jnp.where(lane == LANES - 1, edge - q, up)
        plus_two = jnp.where(
            lane == LANES - 1, edge - down, jnp.where(lane == LANES - 2, edge - up, up_2)
        )
        minus_one = jnp.where(lane == 0, near_0, down)
        minus_two = jnp.where(lane == 0, near_1, jnp.where(lane == 1, near_0, down_2))
        following = jnp.concatenate([q[1:], z_next[c].reshape(1, count_a, LANES)], axis=0)
        preceding = jnp.concatenate([z_prev[c].reshape(1, count_a, LANES), q[:-1]], axis=0)
        right = jnp.where(
            column == count_a - 1,
            a_next[c].reshape(count_z, 1, LANES),
            pltpu.roll(q, count_a - 1, 1),
        )
        left = jnp.where(column == 0, a_prev[c].reshape(count_z, 1, LANES), pltpu.roll(q, 1, 1))
        laplace = (16.0 * (plus_one + minus_one) - 30.0 * q - plus_two - minus_two) / 12.0
        laplace = laplace + (8.0 * (plus_one - minus_one) - plus_two + minus_two) * inverse
        laplace = laplace + geometry * (right + left - 2.0 * q)
        laplace = laplace + (following + preceding - 2.0 * q) / 16.0
        results.append(
            q
            + DIFFUSION[c] * laplace
            - ADVECT * fields[2] * (following - preceding)
            + DT_STEP * (added[c].reshape(shape) + FORCING[c])
        )
    return results


def middle_kernel(
    aspect, gas, added, z_next, z_prev, a_next, a_prev, arrived, partner, cell, dest,
    middle, near_out, gathered, slots, first_z, last_z, first_a, last_a,
):
    count_a = z_next.shape[1]
    count_z = a_next.shape[1]
    near = arrived[partner[0], 2 * SUB :, :]
    results = stencil(gas, added, z_next, z_prev, a_next, a_prev, near, aspect, count_z, count_a)
    for c in range(3):
        middle[c] = results[c].reshape(middle.shape[1:])
    table, turned = gas_table([middle[c] for c in range(3)])
    near_out[...] = jnp.concatenate([t[:2] for t in turned] + [jnp.zeros((2, LANES), F32)], axis=0)
    sample(table, cell, gathered)
    slots[...] = slot_of(dest[...], arrived.shape[0], 2 * LANES)
    edges(middle, first_z, last_z, first_a, last_a, count_z, count_a)


def second_kernel(arrived, near, gathered, slots, out, source, records):
    sectors = arrived.shape[0]
    n = gathered.shape[1]
    for half in range(2):
        fields = [arrived[:, half * SUB + c, :] for c in range(6)]
        now, anchor = fields[:3], fields[3:]
        live = jnp.where(anchor[0] > 0, 1.0, 0.0)
        rows = pl.ds(half, sectors, stride=2)
        change, terms = droplet_rates(now, [gathered[c, rows, :] for c in range(3)], live)
        for c in range(3):
            source[c, rows, :] = terms[c]
            final = 0.75 * anchor[c] + 0.25 * (now[c] + DT_STEP * change[c])
            records[pl.ds(half * SUB + c, sectors, stride=2 * SUB), :] = final
            records[pl.ds(half * SUB + 3 + c, sectors, stride=2 * SUB), :] = anchor[c]
        for c in range(6, SUB):
            records[pl.ds(half * SUB + c, sectors, stride=2 * SUB), :] = jnp.zeros((sectors, LANES), F32)
    placed = place(records, slots, 2 * sectors)
    out[:, : 2 * SUB, :] = placed.reshape(sectors, 2 * SUB, LANES)
    for t in range(sectors):
        out[t, 2 * SUB :, :] = near[...]


def last_kernel(aspect, gas, middle, added, z_next, z_prev, a_next, a_prev, arrived, partner, out, records):
    count_a = z_next.shape[1]
    count_z = a_next.shape[1]
    near = arrived[partner[0], 2 * SUB :, :]
    results = stencil(middle, added, z_next, z_prev, a_next, a_prev, near, aspect, count_z, count_a)
    for c in range(3):
        out[c] = 0.75 * gas[c] + 0.25 * results[c].reshape(out.shape[1:])
    for s in range(arrived.shape[0]):
        for half in range(2):
            at = (2 * s + half) * LANES
            records[:, at : at + LANES] = arrived[s, half * SUB : half * SUB + 6, :]


def kernel(body, outs, scratch=(), smem=(), n_in=0):
    def spec(i):
        return pl.BlockSpec(memory_space=pltpu.SMEM if i in smem else pltpu.VMEM)

    return pl.pallas_call(
        body,
        out_shape=[jax.ShapeDtypeStruct(s, d) for s, d in outs],
        in_specs=[spec(i) for i in range(n_in)],
        out_specs=[pl.BlockSpec(memory_space=pltpu.VMEM) for _ in outs],
        scratch_shapes=list(scratch),
        compiler_params=pltpu.CompilerParams(vmem_limit_bytes=VMEM_LIMIT),
    )


def shifts(first, last, axis):
    count = lax.axis_size(axis)
    ahead = [((i + 1) % count, i) for i in range(count)]
    behind = [(i, (i + 1) % count) for i in range(count)]
    return lax.ppermute(first, axis, ahead), lax.ppermute(last, axis, behind)


def body(gas_fields, drop_mass, drop_temp, drop_speed, dest_first, cell_first, dest_second, cell_second):
    sectors = lax.axis_size("azim")
    _, count_z, count_a, radial = gas_fields.shape
    aspect = count_a * sectors / (2.0 * math.pi * radial)
    cells = count_z * count_a
    n1 = drop_mass.shape[0] // LANES
    n2 = cell_second.shape[0] // LANES
    gas = gas_fields.reshape(3, cells, radial)
    block = (sectors, 3 * SUB, LANES)
    z_edge = ((3, count_a, radial), F32)
    a_edge = ((3, count_z, radial), F32)
    planes = ((3, cells, radial), F32)
    partner = (lax.axis_index("azim") ^ (sectors // 2)).astype(jnp.int32).reshape(1)

    out_1, source_1, first_z, last_z, first_a, last_a = kernel(
        first_kernel,
        [(block, F32), ((3, n1, LANES), F32), z_edge, z_edge, a_edge, a_edge],
        [pltpu.VMEM((3, n1, LANES), F32), pltpu.VMEM((n1, LANES), jnp.int32), pltpu.VMEM((n1 * SUB, LANES), F32)],
        n_in=6,
    )(
        gas,
        drop_mass.reshape(n1, LANES),
        drop_temp.reshape(n1, LANES),
        drop_speed.reshape(n1, LANES),
        cell_first.reshape(n1, LANES),
        dest_first.reshape(n1, LANES),
    )
    arrived_1 = lax.all_to_all(out_1, "azim", split_axis=0, concat_axis=0, tiled=True)
    a_next, a_prev = shifts(first_a, last_a, "azim")
    z_next, z_prev = shifts(first_z, last_z, "axial")
    (added_1,) = kernel(deposit_kernel, [planes], n_in=2)(source_1, cell_first.reshape(n1, LANES))

    cell_2 = cell_second.reshape(n2, LANES)
    middle, near_2, gathered_2, slots_2, first_z, last_z, first_a, last_a = kernel(
        lambda *refs: middle_kernel(aspect, *refs),
        [planes, ((SUB, LANES), F32), ((3, n2, LANES), F32), ((n2, LANES), jnp.int32), z_edge, z_edge, a_edge, a_edge],
        smem=(7,),
        n_in=10,
    )(gas, added_1, z_next, z_prev, a_next, a_prev, arrived_1, partner, cell_2, dest_second.reshape(n2, LANES))
    a_next, a_prev = shifts(first_a, last_a, "azim")
    z_next, z_prev = shifts(first_z, last_z, "axial")

    out_2, source_2 = kernel(
        second_kernel,
        [(block, F32), ((3, n2, LANES), F32)],
        [pltpu.VMEM((n2 * SUB, LANES), F32)],
        n_in=4,
    )(arrived_1, near_2, gathered_2, slots_2)
    arrived_2 = lax.all_to_all(out_2, "azim", split_axis=0, concat_axis=0, tiled=True)
    (added_2,) = kernel(deposit_kernel, [planes], n_in=2)(source_2, cell_2)
    gas_next, drop_records = kernel(
        lambda *refs: last_kernel(aspect, *refs),
        [planes, ((6, n2 * LANES), F32)],
        smem=(8,),
        n_in=9,
    )(gas, middle, added_2, z_next, z_prev, a_next, a_prev, arrived_2, partner)
    return gas_next.reshape(gas_fields.shape), drop_records


def solution(mesh):
    rows = P(("axial", "azim"))
    columns = P(("axial", "azim"), None)
    placed = (P(None, "axial", "azim", None), rows, rows, rows, columns, rows, columns, rows)
    return jax.shard_map(
        body,
        mesh=mesh,
        in_specs=placed,
        out_specs=(P(None, "axial", "azim", None), P(None, ("axial", "azim"))),
        check_vma=False,
    )
```

time: 202 us -> 71.4 us (0.35)
  local copies, waits for them, and re-layouts: 74 us -> 4.42 us
  other arithmetic: 61.5 us -> 0 us
  starting transfers between devices: 61.2 us -> 46.5 us
  Pallas kernels: 0 us -> 11.8 us
  waiting for transfers between devices: 2.41 us -> 7.11 us
    scatter-add x2 -> x0, other arithmetic: 41.5 us -> none  [droplet_terms(): deposit = jnp.zeros_like(flat_gas).at[:, cells].add(source_terms)]
    ppermute x10 -> x8, starting transfers between devices: 50.6 us -> 21.6 us  [shifts(): return (lax.ppermute(first, axis, ahead), lax.ppermute(last, axis, behind))]
    gather x3 -> x0, local copies, waits for them, and re-layouts: 23.6 us -> none  [droplet_terms(): sample_gas = jnp.take(flat_gas, cells, axis=1)]
    scatter x2 -> x0, local copies, waits for them, and re-layouts: 17.6 us -> none  [migrate(): jnp.zeros((components, sectors * capacity), jnp.float32).at[:, position]]
    all_to_all x2, starting transfers between devices: 10.6 us -> 24.9 us  [the longest x1 17.5 us: body(): lax.all_to_all(out_1, 'azim', split_axis=0, concat_axis=0, tiled=True)]
    reshape x4 -> x0, local copies, waits for them, and re-layouts: 13.1 us -> none  [the longest x1 5.26 us: body(): deposit_second.reshape(gas_fields.shape)]
    pallas_call x0 -> x6, Pallas kernels: none -> 11.8 us  [the longest x1 3.03 us: body(): kernel(first_kernel, [(block, F32), ((3, n1, LANES), F32), z_edge, z_edge...]
    another operation x6 -> x0, other arithmetic: 10.3 us -> none
  transfers between devices with their start and end apart: 12 -> 10, of which waited for: 3 -> 2; matrix products, arithmetic and copies ran while one was open for 67% -> 0% of each run, Pallas kernels for 0% -> 4%
where the time goes in v1:
time: 71.4 us; the launch traced here: 70.6 us
  starting transfers between devices  46.5 us (65%)
  Pallas kernels  11.8 us (17%)
  waiting for transfers between devices  7.11 us (10%)
  local copies, waits for them, and re-layouts  4.42 us (6%)
  between operations  0.78 us (1%)
    ppermute x8, starting transfers between devices, shifts(): return (lax.ppermute(first, axis, ahead), lax.ppermute(last, axis, behind))  21.6 us
    all_to_all x1, starting transfers between devices, body(): lax.all_to_all(out_1, 'azim', split_axis=0, concat_axis=0, tiled=True)  17.5 us
    all_to_all x1, starting transfers between devices, body(): lax.all_to_all(out_2, 'azim', split_axis=0, concat_axis=0, tiled=True)  7.42 us
    ppermute x8, waiting for transfers between devices, shifts(): return (lax.ppermute(first, axis, ahead), lax.ppermute(last, axis, behind))  7.1 us
    unnamed x18, local copies, waits for them, and re-layouts  4.42 us
    pallas_call x1, Pallas kernels, body(): kernel(first_kernel, [(block, F32), ((3, n1, LANES), F32), z_edge, z_edge...  3.03 us
    pallas_call x1, Pallas kernels, body(): kernel(second_kernel, [(block, F32), ((3, n2, LANES), F32)], [pltpu.VMEM(...  2.49 us
    pallas_call x1, Pallas kernels, body(): kernel(lambda *refs: middle_kernel(aspect, *refs), [planes, ((SUB, LANES)...  2 us
  transfers between devices with their start and end apart: 10, of which 2 were waited for; matrix products, arithmetic and copies ran while one was open for 0% of the time, Pallas kernels for 4%

profile of v1, /device:TPU:1, one launch (start us, length us, event | category | flops | bytes accessed | tf_op | source)
XLA Modules:
  0.0 70.6 jit_solution(15936138853201490683)
XLA Ops:
  0.6 0.7 copy-done.3
  1.3 0.9 %copy-done = f32[3,16,8,128]{3,2,1,0:T(8,128)S(1)} copy-done((f32[3,16,8,128]{3,2,1,0:T(8,128)S(1)}, f32[3,16,8,128]{3,2,1,0:T(8,128)}, u32[]{:S(2)}) %copy-start) | copy-done | bytes 196632
  2.3 0.7 copy-done.5
  3.0 0.7 copy-done.6
  3.7 0.7 copy-done.7
  4.4 0.7 copy-done.8
  5.0 3.0 %shard_map.95 = (f32[16,24,128]{2,1,0:T(8,128)}, f32[3,16,128]{2,1,0:T(8,128)S(1)}, f32[3,8,128]{2,1,0:T(8,128)S(1)}, f32[3,8,128]{2,1,0:T(8,128)S(1)}, f32[3,16...) custom-call(f32[3,128,128]{2,1,0:T(8,128)S(1)} %bitcast.10, f32[16,128]{1,0:T(8,128)S(1)} %bitcast.18, ...), custom_call_target="tpu_custom_call" | custom-call | tf_op jit(solution)/shard_map/pallas_call | solution.py:328
  8.1 17.5 %all-to-all-start = ((f32[16,24,128]{2,1,0:T(8,128)}), f32[16,24,128]{2,1,0:T(8,128)S(1)}, u32[]{:S(2)}, u32[]{:S(2)}) async-start(f32[16,24,128]{2,1,0:T(8,128)} %get-tuple-element.25), calls=%async_computation | async-start | bytes 393216 | tf_op jit(solution)/shard_map/all_to_all | solution.py:341
  25.6 0.2 collective-permute-start.2
  25.8 1.5 %collective-permute-start.3 = (f32[3,16,128]{2,1,0:T(8,128)S(1)}, f32[3,16,128]{2,1,0:T(8,128)S(1)}, u32[]{:S(2)}, u32[]{:S(2)}) collective-permute-start(f32[3,16,128]{2,1,0:T(8,128)S(1)} %get-tuple-element.24), channel_id=1, source_target_pairs={{0,1},{1,2},{2,3},{3,4},{4,5},{5,6},{6,7},{7,8},{8,9},{9,10},{10,1... | collective-permute-start | bytes 73736 | tf_op jit(solution)/shard_map/ppermute | solution.py:311
  27.3 10.9 %collective-permute-start = (f32[3,8,128]{2,1,0:T(8,128)S(1)}, f32[3,8,128]{2,1,0:T(8,128)S(1)}, u32[]{:S(2)}, u32[]{:S(2)}) collective-permute-start(f32[3,8,128]{2,1,0:T(8,128)S(1)} %get-tuple-element.21), channel_id=1, source_target_pairs={{16,0},{32,16},{48,32},{64,48},{80,64},{96,80},{112,96},{128,112},... | collective-permute-start | bytes 36872 | tf_op jit(solution)/shard_map/ppermute | solution.py:311
  38.3 1.9 %collective-permute-start.1 = (f32[3,8,128]{2,1,0:T(8,128)S(1)}, f32[3,8,128]{2,1,0:T(8,128)S(1)}, u32[]{:S(2)}, u32[]{:S(2)}) collective-permute-start(f32[3,8,128]{2,1,0:T(8,128)S(1)} %get-tuple-element.22), channel_id=1, source_target_pairs={{0,16},{16,32},{32,48},{48,64},{64,80},{80,96},{96,112},{112,128},... | collective-permute-start | bytes 36872 | tf_op jit(solution)/shard_map/ppermute | solution.py:311
  40.2 0.0 copy-start.2
  40.2 0.0 copy-start.4
  40.2 1.1 %shard_map.96.refs_1_ = f32[3,128,128]{2,1,0:T(8,128)S(1)} custom-call(f32[3,16,128]{2,1,0:T(8,128)S(1)} %get-tuple-element.20.source, s32[16,128]{1,0:T(8,128)S(1)} %bitcast.16), custom_call_target="tpu_custom_call" | custom-call | tf_op jit(solution)/shard_map/pallas_call | solution.py:344
  41.3 0.0 collective-permute-done.refs_2_
  41.3 4.7 %collective-permute-done.1.refs_3_ = f32[3,8,128]{2,1,0:T(8,128)S(1)} collective-permute-done((f32[3,8,128]{2,1,0:T(8,128)S(1)}, f32[3,8,128]{2,1,0:T(8,128)S(1)}, u32[]{:S(2)}, u32[]{:S(2)}) %collective-permute-start.1) | collective-permute-done | bytes 12320 | tf_op jit(solution)/shard_map/ppermute | solution.py:311
  46.0 0.0 collective-permute-done.2.refs_4_
  46.0 0.0 collective-permute-done.3.refs_5_
  46.0 0.0 all-to-all-done.refs_6_.arrived
  46.1 2.0 %shard_map.97 = (f32[3,128,128]{2,1,0:T(8,128)S(1)}, f32[8,128]{1,0:T(8,128)S(1)}, f32[3,32,128]{2,1,0:T(8,128)S(1)}, s32[32,128]{1,0:T(8,128)S(1)}, f32[3,8,128...) custom-call(f32[3,128,128]{2,1,0:T(8,128)S(1)} %bitcast.11, ...), custom_call_target="tpu_custom_call" | custom-call | tf_op jit(solution)/shard_map/pallas_call | solution.py:347
  48.1 2.5 %shard_map.98 = (f32[16,24,128]{2,1,0:T(8,128)}, f32[3,32,128]{2,1,0:T(8,128)S(1)}) custom-call(f32[16,24,128]{2,1,0:T(8,128)S(1)} %all-to-all-done.refs_6_.arrived, f32[8,128]{1,0:T(8,128)S(1)} %get-tuple-element.27.near, f32[3,32,128]{2,1,0:T(8,128)S(1)} %get-tuple-element.28.gathered, s32[32,128]{1,0:T(8,128)S(1)} %get-tuple-element.29.slots), custom_call_target="tpu_custom_call" | custom-call | tf_op jit(solution)/shard_map/pallas_call | solution.py:356
  50.6 7.4 %all-to-all-start.1 = ((f32[16,24,128]{2,1,0:T(8,128)}), f32[16,24,128]{2,1,0:T(8,128)S(1)}, u32[]{:S(2)}, u32[]{:S(2)}) async-start(f32[16,24,128]{2,1,0:T(8,128)} %get-tuple-element.35), calls=%async_computation.1 | async-start | bytes 393216 | tf_op jit(solution)/shard_map/all_to_all | solution.py:362
  58.0 0.1 collective-permute-start.6
  58.1 1.6 %collective-permute-start.7 = (f32[3,16,128]{2,1,0:T(8,128)S(1)}, f32[3,16,128]{2,1,0:T(8,128)S(1)}, u32[]{:S(2)}, u32[]{:S(2)}) collective-permute-start(f32[3,16,128]{2,1,0:T(8,128)S(1)} %get-tuple-element.34), channel_id=1, source_target_pairs={{0,1},{1,2},{2,3},{3,4},{4,5},{5,6},{6,7},{7,8},{8,9},{9,10},{10,1... | collective-permute-start | bytes 73736 | tf_op jit(solution)/shard_map/ppermute | solution.py:311
  59.7 1.9 %collective-permute-start.4 = (f32[3,8,128]{2,1,0:T(8,128)S(1)}, f32[3,8,128]{2,1,0:T(8,128)S(1)}, u32[]{:S(2)}, u32[]{:S(2)}) collective-permute-start(f32[3,8,128]{2,1,0:T(8,128)S(1)} %get-tuple-element.31), channel_id=1, source_target_pairs={{16,0},{32,16},{48,32},{64,48},{80,64},{96,80},{112,96},{128,112},... | collective-permute-start | bytes 36872 | tf_op jit(solution)/shard_map/ppermute | solution.py:311
  61.6 3.4 %collective-permute-start.5 = (f32[3,8,128]{2,1,0:T(8,128)S(1)}, f32[3,8,128]{2,1,0:T(8,128)S(1)}, u32[]{:S(2)}, u32[]{:S(2)}) collective-permute-start(f32[3,8,128]{2,1,0:T(8,128)S(1)} %get-tuple-element.32), channel_id=1, source_target_pairs={{0,16},{16,32},{32,48},{48,64},{64,80},{80,96},{96,112},{112,128},... | collective-permute-start | bytes 36872 | tf_op jit(solution)/shard_map/ppermute | solution.py:311
  65.0 2.0 %shard_map.99.refs_2_ = f32[3,128,128]{2,1,0:T(8,128)S(1)} custom-call(f32[3,32,128]{2,1,0:T(8,128)S(1)} %get-tuple-element.30.source, s32[32,128]{1,0:T(8,128)S(1)} %bitcast.14), custom_call_target="tpu_custom_call" | custom-call | tf_op jit(solution)/shard_map/pallas_call | solution.py:363
  67.0 0.0 collective-permute-done.4.refs_3_
  67.0 2.4 %collective-permute-done.5.refs_4_ = f32[3,8,128]{2,1,0:T(8,128)S(1)} collective-permute-done((f32[3,8,128]{2,1,0:T(8,128)S(1)}, f32[3,8,128]{2,1,0:T(8,128)S(1)}, u32[]{:S(2)}, u32[]{:S(2)}) %collective-permute-start.5) | collective-permute-done | bytes 12320 | tf_op jit(solution)/shard_map/ppermute | solution.py:311
  69.4 0.0 collective-permute-done.6.refs_5_
  69.4 1.2 %shard_map.100 = (f32[3,128,128]{2,1,0:T(8,128)}, f32[6,4096]{1,0:T(8,128)}) custom-call(f32[3,128,128]{2,1,0:T(8,128)S(1)} %bitcast.12, f32[3,128,128]{2,1,0:T(8,128)S(1)} %get-tuple-element.26.refs_1_, f32[3,128,128]{2,1,0:T(8,128)S(1)} %shard_map.99.refs_2_, f32[3,8,128]{2,1,0:T(8,128)S(1)} %collective-permute-done.4.refs_3_, ...), custom_call_target="tpu_custom_call" | custom-call | tf_op jit(solution)/shard_map/pallas_call | solution.py:364
  (12 shorter events, 0.0 us)
Async XLA Ops:
  0.6 0.7 copy-start.3
  1.3 0.9 %copy-start = (f32[3,16,8,128]{3,2,1,0:T(8,128)S(1)}, f32[3,16,8,128]{3,2,1,0:T(8,128)}, u32[]{:S(2)}) copy-start(f32[3,16,8,128]{3,2,1,0:T(8,128)} %param.8) | copy-start | bytes 589828
  2.3 0.7 copy-start.5
  3.0 0.7 copy-start.6
  3.7 0.7 copy-start.7
  4.3 0.7 copy-start.8
  8.1 37.9 %all-to-all-start = ((f32[16,24,128]{2,1,0:T(8,128)}), f32[16,24,128]{2,1,0:T(8,128)S(1)}, u32[]{:S(2)}, u32[]{:S(2)}) async-start(f32[16,24,128]{2,1,0:T(8,128)} %get-tuple-element.25), calls=%async_computation | async-start | bytes 393216 | tf_op jit(solution)/shard_map/all_to_all | solution.py:341
  25.5 20.5 %copy-start.1 = (f32[3,16,8,128]{3,2,1,0:T(8,128)S(1)}, f32[3,16,8,128]{3,2,1,0:T(8,128)}, u32[]{:S(2)}) copy-start(f32[3,16,8,128]{3,2,1,0:T(8,128)} %param.8) | copy-start | bytes 589828
  25.6 20.5 %collective-permute-start.2 = (f32[3,16,128]{2,1,0:T(8,128)S(1)}, f32[3,16,128]{2,1,0:T(8,128)S(1)}, u32[]{:S(2)}, u32[]{:S(2)}) collective-permute-start(f32[3,16,128]{2,1,0:T(8,128)S(1)} %get-tuple-element.23), channel_id=1, source_target_pairs={{1,0},{2,1},{3,2},{4,3},{5,4},{6,5},{7,6},{8,7},{9,8},{10,9},{11,1... | collective-permute-start | bytes 73736 | tf_op jit(solution)/shard_map/ppermute | solution.py:311
  25.8 20.2 %collective-permute-start.3 = (f32[3,16,128]{2,1,0:T(8,128)S(1)}, f32[3,16,128]{2,1,0:T(8,128)S(1)}, u32[]{:S(2)}, u32[]{:S(2)}) collective-permute-start(f32[3,16,128]{2,1,0:T(8,128)S(1)} %get-tuple-element.24), channel_id=1, source_target_pairs={{0,1},{1,2},{2,3},{3,4},{4,5},{5,6},{6,7},{7,8},{8,9},{9,10},{10,1... | collective-permute-start | bytes 73736 | tf_op jit(solution)/shard_map/ppermute | solution.py:311
  27.3 14.0 %collective-permute-start = (f32[3,8,128]{2,1,0:T(8,128)S(1)}, f32[3,8,128]{2,1,0:T(8,128)S(1)}, u32[]{:S(2)}, u32[]{:S(2)}) collective-permute-start(f32[3,8,128]{2,1,0:T(8,128)S(1)} %get-tuple-element.21), channel_id=1, source_target_pairs={{16,0},{32,16},{48,32},{64,48},{80,64},{96,80},{112,96},{128,112},... | collective-permute-start | bytes 36872 | tf_op jit(solution)/shard_map/ppermute | solution.py:311
  38.3 7.8 %collective-permute-start.1 = (f32[3,8,128]{2,1,0:T(8,128)S(1)}, f32[3,8,128]{2,1,0:T(8,128)S(1)}, u32[]{:S(2)}, u32[]{:S(2)}) collective-permute-start(f32[3,8,128]{2,1,0:T(8,128)S(1)} %get-tuple-element.22), channel_id=1, source_target_pairs={{0,16},{16,32},{32,48},{48,64},{64,80},{80,96},{96,112},{112,128},... | collective-permute-start | bytes 36872 | tf_op jit(solution)/shard_map/ppermute | solution.py:311
  40.2 5.9 %copy-start.2 = (s32[4096]{0:T(1024)S(1)}, s32[4096]{0:T(1024)}, u32[]{:S(2)}) copy-start(s32[4096]{0:T(1024)} %param.15) | copy-start | bytes 49156
  40.2 5.8 %copy-start.4 = (s32[4096,1]{0,1:T(1,128)S(1)}, s32[4096,1]{0,1:T(1,128)}, u32[]{:S(2)}) copy-start(s32[4096,1]{0,1:T(1,128)} %param.14) | copy-start | bytes 49156
  50.6 18.9 %all-to-all-start.1 = ((f32[16,24,128]{2,1,0:T(8,128)}), f32[16,24,128]{2,1,0:T(8,128)S(1)}, u32[]{:S(2)}, u32[]{:S(2)}) async-start(f32[16,24,128]{2,1,0:T(8,128)} %get-tuple-element.35), calls=%async_computation.1 | async-start | bytes 393216 | tf_op jit(solution)/shard_map/all_to_all | solution.py:362
  58.0 11.4 %collective-permute-start.6 = (f32[3,16,128]{2,1,0:T(8,128)S(1)}, f32[3,16,128]{2,1,0:T(8,128)S(1)}, u32[]{:S(2)}, u32[]{:S(2)}) collective-permute-start(f32[3,16,128]{2,1,0:T(8,128)S(1)} %get-tuple-element.33), channel_id=1, source_target_pairs={{1,0},{2,1},{3,2},{4,3},{5,4},{6,5},{7,6},{8,7},{9,8},{10,9},{11,1... | collective-permute-start | bytes 73736 | tf_op jit(solution)/shard_map/ppermute | solution.py:311
  58.1 11.3 %collective-permute-start.7 = (f32[3,16,128]{2,1,0:T(8,128)S(1)}, f32[3,16,128]{2,1,0:T(8,128)S(1)}, u32[]{:S(2)}, u32[]{:S(2)}) collective-permute-start(f32[3,16,128]{2,1,0:T(8,128)S(1)} %get-tuple-element.34), channel_id=1, source_target_pairs={{0,1},{1,2},{2,3},{3,4},{4,5},{5,6},{6,7},{7,8},{8,9},{9,10},{10,1... | collective-permute-start | bytes 73736 | tf_op jit(solution)/shard_map/ppermute | solution.py:311
  59.7 7.3 %collective-permute-start.4 = (f32[3,8,128]{2,1,0:T(8,128)S(1)}, f32[3,8,128]{2,1,0:T(8,128)S(1)}, u32[]{:S(2)}, u32[]{:S(2)}) collective-permute-start(f32[3,8,128]{2,1,0:T(8,128)S(1)} %get-tuple-element.31), channel_id=1, source_target_pairs={{16,0},{32,16},{48,32},{64,48},{80,64},{96,80},{112,96},{128,112},... | collective-permute-start | bytes 36872 | tf_op jit(solution)/shard_map/ppermute | solution.py:311
  61.6 7.8 %collective-permute-start.5 = (f32[3,8,128]{2,1,0:T(8,128)S(1)}, f32[3,8,128]{2,1,0:T(8,128)S(1)}, u32[]{:S(2)}, u32[]{:S(2)}) collective-permute-start(f32[3,8,128]{2,1,0:T(8,128)S(1)} %get-tuple-element.32), channel_id=1, source_target_pairs={{0,16},{16,32},{32,48},{48,64},{64,80},{80,96},{96,112},{112,128},... | collective-permute-start | bytes 36872 | tf_op jit(solution)/shard_map/ppermute | solution.py:311

commit v2 on v1

v2 whole, which is shorter than its diff:
```python
import math

import jax
import jax.numpy as jnp
from jax import lax
from jax.experimental import pallas as pl
from jax.experimental.pallas import tpu as pltpu
from jax.sharding import PartitionSpec as P

DT_STEP = 0.01
TAU_HEAT = 0.04
TAU_MASS = 0.05
TAU_DRAG = 0.03
LATENT = 0.5
COUPLING = 1.0
FORCING = (0.0, 0.0, 4.0)
ADVECT = 0.16
RADIUS_FLOOR = 0.7
DIFFUSION = (0.2, 0.15, 0.17)
WALL_VALUES = (1.0, 0.0, 0.0)

F32 = jnp.float32
BF16 = jnp.bfloat16
LANES = 128
SUB = 8
VMEM_LIMIT = 40 << 20
WHOLE_VMEM = 60 << 20
COST_SCALE = 1.0


def iota(shape, dim):
    return lax.broadcasted_iota(jnp.int32, shape, dim)


def one_hot(row, size):
    hit = iota((size, row.shape[1]), 0) == row
    return jnp.where(hit, 1.0, 0.0).astype(BF16)


def halves(x):
    head = x.astype(BF16)
    return head, (x - head.astype(F32)).astype(BF16)


def wide_row(ref, j):
    return jnp.concatenate([ref[pl.ds(j, 1), :], ref[pl.ds(j + 1, 1), :]], axis=1)


def dot_nt(a, b):
    return lax.dot_general(a, b, (((1,), (1,)), ((), ())), preferred_element_type=F32)


def gas_table(planes):
    turned = [p.T for p in planes]
    parts = [jnp.concatenate(halves(t), axis=1) for t in turned]
    return jnp.concatenate(parts, axis=0), turned


def sample(table, cell_ref, out_ref):
    size = table.shape[1] // 2
    lanes_r = table.shape[0] // 3
    shift = lanes_r.bit_length() - 1
    for j in range(0, cell_ref.shape[0], 2):
        cell = wide_row(cell_ref, j)
        pick = one_hot(cell >> shift, size)
        mixed = jnp.dot(table, jnp.concatenate([pick, pick], axis=0), preferred_element_type=F32)
        here = iota((lanes_r, cell.shape[1]), 0) == (cell & (lanes_r - 1))
        for c in range(3):
            part = jnp.where(here, mixed[c * lanes_r : (c + 1) * lanes_r], 0.0)
            row = jnp.sum(part, axis=0, keepdims=True)
            out_ref[c, pl.ds(j, 1), :] = row[:, :LANES]
            out_ref[c, pl.ds(j + 1, 1), :] = row[:, LANES:]


def droplet_rates(states, gas, live):
    mass, temp, speed = states
    excess = 0.3 + 0.2 * jnp.tanh(temp) - gas[1]
    evaporate = mass * excess / TAU_MASS
    heating = gas[0] - temp
    drag = gas[2] - speed
    change = (
        -evaporate * live,
        (heating / TAU_HEAT - LATENT * excess / TAU_MASS) * live,
        drag / TAU_DRAG * live,
    )
    source = (
        -COUPLING * mass * heating / TAU_HEAT,
        COUPLING * evaporate,
        -COUPLING * mass * drag / TAU_DRAG,
    )
    return change, source


def deposit(source_ref, cell_ref, rows, lanes_r):
    shift = lanes_r.bit_length() - 1
    low = lanes_r // 2
    total = None
    for j in range(0, cell_ref.shape[0], 2):
        cell = wide_row(cell_ref, j)
        column = jnp.where((cell & low) > 0, rows, 0) + (cell >> shift)
        here = iota((low, cell.shape[1]), 0) == (cell & (low - 1))
        pairs = [halves(wide_row(source_ref.at[c], j)) for c in range(3)]
        spread = [
            jnp.where(here, pairs[c][part].astype(F32), 0.0) for part in range(2) for c in range(3)
        ]
        piece = dot_nt(jnp.concatenate(spread, axis=0).astype(BF16), one_hot(column, 2 * rows))
        total = piece if total is None else total + piece
    total = total[: 3 * low] + total[3 * low :]
    planes = [total[c * low : (c + 1) * low] for c in range(3)]
    return [jnp.concatenate([p[:, :rows], p[:, rows:]], axis=0).T for p in planes]


def slot_of(dest, sectors, capacity):
    n = dest.shape[0]
    hits = jnp.concatenate(
        [jnp.where(dest == t, 1.0, 0.0) for t in range(sectors)], axis=0
    ).astype(BF16)
    upto = jnp.where(iota((LANES, LANES), 0) <= iota((LANES, LANES), 1), 1.0, 0.0).astype(BF16)
    inside = jnp.dot(hits, upto, preferred_element_type=F32)
    every = jnp.dot(hits, jnp.ones((LANES, LANES), BF16), preferred_element_type=F32)
    before = jnp.where(iota((n, n), 1) < iota((n, n), 0), 1.0, 0.0).astype(BF16)
    rank = jnp.zeros(dest.shape, F32)
    for t in range(sectors):
        rows = slice(t * n, (t + 1) * n)
        carry = jnp.dot(before, every[rows].astype(BF16), preferred_element_type=F32)
        rank = rank + jnp.where(dest == t, inside[rows] + carry, 0.0)
    return dest * capacity + rank.astype(jnp.int32) - 1


def place(record_ref, slot_ref, out_ref):
    sectors = out_ref.shape[0]
    capacity = 2 * LANES
    total = None
    for j in range(0, slot_ref.shape[0], 2):
        slot = wide_row(slot_ref, j)
        sector = slot >> (capacity.bit_length() - 1)
        record = jnp.concatenate(
            [record_ref[pl.ds(SUB * j, SUB), :], record_ref[pl.ds(SUB * (j + 1), SUB), :]], axis=1
        )
        spread = [
            jnp.where(sector == t, part.astype(F32), 0.0)
            for part in halves(record)
            for t in range(sectors)
        ]
        piece = dot_nt(
            jnp.concatenate(spread, axis=0).astype(BF16), one_hot(slot & (capacity - 1), capacity)
        )
        total = piece if total is None else total + piece
    count = sectors * SUB
    total = total[:count] + total[count:]
    out_ref[:, :SUB, :] = total[:, :LANES].reshape(sectors, SUB, LANES)
    out_ref[:, SUB : 2 * SUB, :] = total[:, LANES:].reshape(sectors, SUB, LANES)


def near_rows(turned):
    return jnp.concatenate([t[:2] for t in turned] + [jnp.zeros((2, LANES), F32)], axis=0)


def send_near(out_ref, near):
    for t in range(out_ref.shape[0]):
        out_ref[t, 2 * SUB :, :] = near


def columns_of(ref, c, at, count_z, count_a):
    return ref[c, pl.ds(at, count_z, stride=count_a), :]


def first_kernel(
    gas_hbm, mass_hbm, temp_hbm, speed_hbm, cell_hbm, dest_hbm,
    out, source, first_a, last_a,
    gas, mass, temp, speed, cell, dest, sems, gathered, slots, records,
):
    sectors = out.shape[0]
    count_z = first_a.shape[1]
    count_a = gas.shape[1] // count_z
    loads = [
        pltpu.make_async_copy(a, b, sems.at[i])
        for i, (a, b) in enumerate(
            (
                (dest_hbm, dest),
                (gas_hbm, gas),
                (cell_hbm, cell),
                (mass_hbm, mass),
                (temp_hbm, temp),
                (speed_hbm, speed),
            )
        )
    ]
    for load in loads:
        load.start()
    records[...] = jnp.zeros(records.shape, F32)
    loads[0].wait()
    slots[...] = slot_of(dest[...], sectors, 2 * LANES)
    for load in loads[1:]:
        load.wait()
    table, turned = gas_table([gas[c] for c in range(3)])
    send_near(out, near_rows(turned))
    sample(table, cell, gathered)
    states = (mass[...], temp[...], speed[...])
    live = jnp.where(states[0] > 0, 1.0, 0.0)
    change, terms = droplet_rates(states, [gathered[c] for c in range(3)], live)
    n = cell.shape[0]
    for c in range(3):
        source[c] = terms[c]
        records[pl.ds(c, n, stride=SUB), :] = states[c] + DT_STEP * change[c]
        records[pl.ds(3 + c, n, stride=SUB), :] = states[c]
    place(records, slots, out)
    for c in range(3):
        first_a[c] = columns_of(gas, c, 0, count_z, count_a)
        last_a[c] = columns_of(gas, c, count_a - 1, count_z, count_a)


def first_deposit_kernel(sectors, count_a, source, cell, gas, dest, out, far_z, near_z, slots):
    total = deposit(source, cell, out.shape[1], out.shape[2])
    end = out.shape[1]
    even = (lax.axis_index("axial") & 1) == 0
    for c in range(3):
        out[c] = total[c]
        first = [gas[c, :count_a, :], gas[c, count_a : 2 * count_a, :], total[c][:count_a]]
        last = [
            gas[c, end - count_a :, :],
            gas[c, end - 2 * count_a : end - count_a, :],
            total[c][end - count_a :],
        ]
        for i in range(3):
            near_z[3 * c + i] = jnp.where(even, last[i], first[i])
            far_z[3 * c + i] = jnp.where(even, first[i], last[i])
    slots[...] = slot_of(dest[...], sectors, 2 * LANES)


def stencil(fields, following, preceding, right_edge, left_edge, near, added, aspect):
    shape = fields[0].shape
    count_a = shape[1]
    pos = iota((1, 1, LANES), 2).astype(F32) + 0.5
    inverse = 1.0 / (12.0 * pos)
    geometry = aspect * aspect / jnp.maximum(pos / LANES, RADIUS_FLOOR) ** 2
    lane = iota(shape, 2)
    column = iota(shape, 1)
    results = []
    for c in range(3):
        q = fields[c]
        edge = 2.0 * WALL_VALUES[c]
        near_0, near_1 = near[c]
        up = pltpu.roll(q, LANES - 1, 2)
        down = pltpu.roll(q, 1, 2)
        up_2 = pltpu.roll(q, LANES - 2, 2)
        down_2 = pltpu.roll(q, 2, 2)
        plus_one = jnp.where(lane == LANES - 1, edge - q, up)
        plus_two = jnp.where(
            lane == LANES - 1, edge - down, jnp.where(lane == LANES - 2, edge - up, up_2)
        )
        minus_one = jnp.where(lane == 0, near_0, down)
        minus_two = jnp.where(lane == 0, near_1, jnp.where(lane == 1, near_0, down_2))
        right = jnp.where(column == count_a - 1, right_edge[c], pltpu.roll(q, count_a - 1, 1))
        left = jnp.where(column == 0, left_edge[c], pltpu.roll(q, 1, 1))
        laplace = (16.0 * (plus_one + minus_one) - 30.0 * q - plus_two - minus_two) / 12.0
        laplace = laplace + (8.0 * (plus_one - minus_one) - plus_two + minus_two) * inverse
        laplace = laplace + geometry * (right + left - 2.0 * q)
        laplace = laplace + (following[c] + preceding[c] - 2.0 * q) / 16.0
        results.append(
            q
            + DIFFUSION[c] * laplace
            - ADVECT * fields[2] * (following[c] - preceding[c])
            + DT_STEP * (added[c] + FORCING[c])
        )
    return results


def between(q, z_prev, z_next):
    return (
        jnp.concatenate([q[1:], z_next[None]], axis=0),
        jnp.concatenate([z_prev[None], q[:-1]], axis=0),
    )


def near_columns(near):
    return jnp.concatenate([near, jnp.zeros((LANES - SUB, LANES), F32)], axis=0).T


def column_blocks(across, count_z, count_a):
    return [
        [across[:, 2 * c + i : 2 * c + i + 1].reshape(count_z, count_a, 1) for i in range(2)]
        for c in range(3)
    ]


def across_axis(sectors):
    return lax.axis_index("azim") ^ (sectors // 2)


def outer_planes(near_z, far_z):
    even = (lax.axis_index("axial") & 1) == 0
    count = range(near_z.shape[0])
    return (
        [jnp.where(even, near_z[i], far_z[i]) for i in count],
        [jnp.where(even, far_z[i], near_z[i]) for i in count],
    )


def middle_kernel(
    aspect, gas, added, far_z, near_z, a_next, a_prev, arrived,
    middle, near, first_a, last_a,
):
    count_z, count_a = a_next.shape[1], near_z.shape[1]
    shape = (count_z, count_a, LANES)
    z_next, z_prev = outer_planes(near_z, far_z)
    across = near_columns(arrived[across_axis(arrived.shape[0]), 2 * SUB :, :])
    fields = [gas[c].reshape(shape) for c in range(3)]
    pairs = [between(fields[c], z_prev[3 * c], z_next[3 * c]) for c in range(3)]
    results = stencil(
        fields,
        [p[0] for p in pairs],
        [p[1] for p in pairs],
        [a_next[c].reshape(count_z, 1, LANES) for c in range(3)],
        [a_prev[c].reshape(count_z, 1, LANES) for c in range(3)],
        column_blocks(across, count_z, count_a),
        [added[c].reshape(shape) for c in range(3)],
        aspect,
    )
    for c in range(3):
        middle[c] = results[c].reshape(middle.shape[1:])
    outer = [planes[3 * c] for c in range(3) for planes in (z_prev, z_next)]
    for i, plane in enumerate(outer):
        first_a[3 * count_z + i] = plane[0]
        last_a[3 * count_z + i] = plane[count_a - 1]
    for c in range(3):
        first_a[c * count_z : (c + 1) * count_z] = columns_of(middle, c, 0, count_z, count_a)
        last_a[c * count_z : (c + 1) * count_z] = columns_of(middle, c, count_a - 1, count_z, count_a)
    unused = first_a.shape[0] - 3 * count_z - len(outer)
    first_a[3 * count_z + len(outer) :] = jnp.zeros((unused, LANES), F32)
    last_a[3 * count_z + len(outer) :] = jnp.zeros((unused, LANES), F32)
    rest = jnp.zeros((LANES - len(outer) * count_a, LANES), F32)
    near[...] = jnp.concatenate(outer + [rest], axis=0).T[:2]


def sample_kernel(middle, outer_near, cell, gathered, near):
    table, turned = gas_table([middle[c] for c in range(3)])
    sample(table, cell, gathered)
    near[...] = jnp.concatenate([t[:2] for t in turned] + [outer_near[...]], axis=0)


def second_kernel(gathered, near, arrived, slots, a_next, a_prev, out, source, records):
    del a_next, a_prev
    send_near(out, near[...])
    sectors = arrived.shape[0]
    for half in range(2):
        values = [arrived[:, half * SUB + c, :] for c in range(6)]
        now, anchor = values[:3], values[3:]
        live = jnp.where(anchor[0] > 0, 1.0, 0.0)
        rows = pl.ds(half, sectors, stride=2)
        change, terms = droplet_rates(now, [gathered[c, rows, :] for c in range(3)], live)
        for c in range(3):
            source[c, rows, :] = terms[c]
            final = 0.75 * anchor[c] + 0.25 * (now[c] + DT_STEP * change[c])
            records[pl.ds(half * SUB + c, sectors, stride=2 * SUB), :] = final
            records[pl.ds(half * SUB + 3 + c, sectors, stride=2 * SUB), :] = anchor[c]
        for c in range(6, SUB):
            records[pl.ds(half * SUB + c, sectors, stride=2 * SUB), :] = jnp.zeros((sectors, LANES), F32)
    place(records, slots, out)


def last_kernel(aspect, gas, middle, source, cell, far_z, near_z, a_next, a_prev, arrived, out, records):
    added = deposit(source, cell, gas.shape[1], gas.shape[2])
    count_a = near_z.shape[1]
    z_next, z_prev = outer_planes(near_z, far_z)
    count_z = gas.shape[1] // count_a
    shape = (count_z, count_a, LANES)
    end = gas.shape[1]
    across = near_columns(arrived[across_axis(arrived.shape[0]), 2 * SUB :, :])
    own = count_z * 3

    def outer(before, after):
        return jnp.concatenate([before[None], after[None]], axis=0)

    def outer_rows(ref, c):
        return ref[own + 2 * c : own + 2 * c + 2, :].reshape(2, 1, LANES)

    halo = stencil(
        [outer(z_prev[3 * c], z_next[3 * c]) for c in range(3)],
        [outer(gas[c, :count_a, :], z_next[3 * c + 1]) for c in range(3)],
        [outer(z_prev[3 * c + 1], gas[c, end - count_a :, :]) for c in range(3)],
        [outer_rows(a_next, c) for c in range(3)],
        [outer_rows(a_prev, c) for c in range(3)],
        [
            [
                across[2 * c * count_a : 2 * (c + 1) * count_a, 6 + i : 7 + i].reshape(2, count_a, 1)
                for i in range(2)
            ]
            for c in range(3)
        ],
        [outer(z_prev[3 * c + 2], z_next[3 * c + 2]) for c in range(3)],
        aspect,
    )
    fields = [middle[c].reshape(shape) for c in range(3)]
    pairs = [between(fields[c], halo[c][0], halo[c][1]) for c in range(3)]
    results = stencil(
        fields,
        [p[0] for p in pairs],
        [p[1] for p in pairs],
        [a_next[c * count_z : (c + 1) * count_z, :].reshape(count_z, 1, LANES) for c in range(3)],
        [a_prev[c * count_z : (c + 1) * count_z, :].reshape(count_z, 1, LANES) for c in range(3)],
        column_blocks(across, count_z, count_a),
        [added[c].reshape(shape) for c in range(3)],
        aspect,
    )
    for c in range(3):
        out[c] = 0.75 * gas[c] + 0.25 * results[c].reshape(out.shape[1:])
    for s in range(arrived.shape[0]):
        for half in range(2):
            at = (2 * s + half) * LANES
            records[:, at : at + LANES] = arrived[s, half * SUB : half * SUB + 6, :]


def kernel(body, outs, scratch=(), smem=(), n_in=0, home=pltpu.VMEM, limit=VMEM_LIMIT, cost=1.0):
    def spec(i):
        return pl.BlockSpec(memory_space=pltpu.SMEM if i in smem else home)

    return pl.pallas_call(
        body,
        out_shape=[jax.ShapeDtypeStruct(s, d) for s, d in outs],
        in_specs=[spec(i) for i in range(n_in)],
        out_specs=[pl.BlockSpec(memory_space=pltpu.VMEM) for _ in outs],
        scratch_shapes=list(scratch),
        compiler_params=pltpu.CompilerParams(vmem_limit_bytes=limit),
        cost_estimate=pl.CostEstimate(flops=int(cost * 1e9 * COST_SCALE), bytes_accessed=0, transcendentals=0),
    )


def shifts(first, last, axis):
    count = lax.axis_size(axis)
    ahead = [((i + 1) % count, i) for i in range(count)]
    behind = [(i, (i + 1) % count) for i in range(count)]
    return lax.ppermute(first, axis, ahead), lax.ppermute(last, axis, behind)


def swaps(near, far, axis):
    count = lax.axis_size(axis)
    odd = [(i, (i + (1 if i % 2 else -1)) % count) for i in range(count)]
    even = [(i, i ^ 1) for i in range(count)]
    near = lax.ppermute(near, axis, even)
    return lax.ppermute(far, axis, odd), near


def body(gas_fields, drop_mass, drop_temp, drop_speed, dest_first, cell_first, dest_second, cell_second):
    sectors = lax.axis_size("azim")
    _, count_z, count_a, radial = gas_fields.shape
    aspect = count_a * sectors / (2.0 * math.pi * radial)
    cells = count_z * count_a
    n1 = drop_mass.shape[0] // LANES
    n2 = cell_second.shape[0] // LANES
    gas = gas_fields.reshape(3, cells, radial)
    block = (sectors, 3 * SUB, LANES)
    z_edge = ((9, count_a, radial), F32)
    a_edge = ((3, count_z, radial), F32)
    a_edge_2 = ((-(-(3 * count_z + 6) // SUB) * SUB, radial), F32)
    planes = ((3, cells, radial), F32)
    cell_1 = cell_first.reshape(n1, LANES)
    cell_2 = cell_second.reshape(n2, LANES)

    out_1, source_1, first_a, last_a = kernel(
        first_kernel,
        [(block, F32), ((3, n1, LANES), F32), a_edge, a_edge],
        [pltpu.VMEM((3, cells, radial), F32)]
        + [pltpu.VMEM((n1, LANES), F32)] * 3
        + [pltpu.VMEM((n1, LANES), jnp.int32)] * 2
        + [pltpu.SemaphoreType.DMA((6,))]
        + [pltpu.VMEM((3, n1, LANES), F32), pltpu.VMEM((n1, LANES), jnp.int32), pltpu.VMEM((n1 * SUB, LANES), F32)],
        n_in=6,
        home=pltpu.HBM,
        limit=WHOLE_VMEM,
        cost=3.0,
    )(
        gas,
        drop_mass.reshape(n1, LANES),
        drop_temp.reshape(n1, LANES),
        drop_speed.reshape(n1, LANES),
        cell_1,
        dest_first.reshape(n1, LANES),
    )
    arrived_1 = lax.all_to_all(out_1, "azim", split_axis=0, concat_axis=0, tiled=True)
    a_next, a_prev = shifts(first_a, last_a, "azim")
    added_1, far_z, near_z, slots_2 = kernel(
        lambda *refs: first_deposit_kernel(sectors, count_a, *refs),
        [planes, z_edge, z_edge, ((n2, LANES), jnp.int32)],
        n_in=4,
        cost=1.4,
    )(source_1, cell_1, gas, dest_second.reshape(n2, LANES))
    far_z, near_z = swaps(near_z, far_z, "axial")

    middle, outer_near, first_a, last_a = kernel(
        lambda *refs: middle_kernel(aspect, *refs),
        [planes, ((2, LANES), F32), a_edge_2, a_edge_2],
        n_in=7,
    )(gas, added_1, far_z, near_z, a_next, a_prev, arrived_1)
    a_next, a_prev = shifts(first_a, last_a, "azim")
    gathered_2, near_2 = kernel(
        sample_kernel, [((3, n2, LANES), F32), ((SUB, LANES), F32)], n_in=3, cost=1.2
    )(middle, outer_near, cell_2)
    out_2, source_2 = kernel(
        second_kernel,
        [(block, F32), ((3, n2, LANES), F32)],
        [pltpu.VMEM((n2 * SUB, LANES), F32)],
        n_in=6,
        cost=2.4,
    )(gathered_2, near_2, arrived_1, slots_2, a_next, a_prev)
    arrived_2 = lax.all_to_all(out_2, "azim", split_axis=0, concat_axis=0, tiled=True)
    gas_next, drop_records = kernel(
        lambda *refs: last_kernel(aspect, *refs),
        [planes, ((6, n2 * LANES), F32)],
        n_in=9,
        cost=1.8,
    )(gas, middle, source_2, cell_2, far_z, near_z, a_next, a_prev, arrived_2)
    return gas_next.reshape(gas_fields.shape), drop_records


def solution(mesh):
    rows = P(("axial", "azim"))
    columns = P(("axial", "azim"), None)
    placed = (P(None, "axial", "azim", None), rows, rows, rows, columns, rows, columns, rows)
    return jax.shard_map(
        body,
        mesh=mesh,
        in_specs=placed,
        out_specs=(P(None, "axial", "azim", None), P(None, ("axial", "azim"))),
        check_vma=False,
    )
```

time: 71.4 us -> 66.1 us (0.926)
  blocking collectives: 0 us -> 17.7 us
  starting transfers between devices: 46.5 us -> 36.2 us
  waiting for transfers between devices: 7.11 us -> 1.79 us
  local copies, waits for them, and re-layouts: 4.42 us -> 0.04 us
  Pallas kernels: 11.8 us -> 9.22 us
    all_to_all x0 -> x1, blocking collectives: none -> 17.7 us  [body(): lax.all_to_all(out_2, 'azim', split_axis=0, concat_axis=0, tiled=True)]
    ppermute x8 -> x4, starting transfers between devices: 21.6 us -> 5.68 us  [shifts(): return (lax.ppermute(first, axis, ahead), lax.ppermute(last, axis, behind))]
    ppermute x0 -> x2, starting transfers between devices: none -> 12.9 us  [the longest x1 11 us: swaps(): return (lax.ppermute(far, axis, odd), near)]
    all_to_all x1 -> x0, starting transfers between devices: 7.42 us -> none  [body(): lax.all_to_all(out_2, 'azim', split_axis=0, concat_axis=0, tiled=True)]
    ppermute x8 -> x4, waiting for transfers between devices: 7.1 us -> 1.78 us  [shifts(): return (lax.ppermute(first, axis, ahead), lax.ppermute(last, axis, behind))]
    unnamed x18 -> x14, local copies, waits for them, and re-layouts: 4.42 us -> 0.04 us
    pallas_call x4, Pallas kernels: 8.1 us -> 5.97 us  [the longest x1 3.17 us: body(): kernel(first_kernel, [(block, F32), ((3, n1, LANES), F32), a_edge, a_edge...]
    pallas_call x1, Pallas kernels: 2.49 us -> 1.33 us  [body(): kernel(second_kernel, [(block, F32), ((3, n2, LANES), F32)], [pltpu.VMEM(...]
  transfers between devices with their start and end apart: 10 -> 7, of which waited for: 2 -> 1; matrix products, arithmetic and copies ran while one was open for 0% -> 0% of each run, Pallas kernels for 4% -> 3%
where the time goes in v2:
time: 66.1 us; the launch traced here: 65.7 us
  starting transfers between devices  36.2 us (55%)
  blocking collectives  17.7 us (27%)
  Pallas kernels  9.22 us (14%)
  waiting for transfers between devices  1.79 us (3%)
  between operations  0.79 us (1%)
    all_to_all x1, blocking collectives, body(): lax.all_to_all(out_2, 'azim', split_axis=0, concat_axis=0, tiled=True)  17.7 us
    all_to_all x1, starting transfers between devices, body(): lax.all_to_all(out_1, 'azim', split_axis=0, concat_axis=0, tiled=True)  17.6 us
    ppermute x1, starting transfers between devices, swaps(): return (lax.ppermute(far, axis, odd), near)  11 us
    ppermute x4, starting transfers between devices, shifts(): return (lax.ppermute(first, axis, ahead), lax.ppermute(last, axis, behind))  5.68 us
    pallas_call x1, Pallas kernels, body(): kernel(first_kernel, [(block, F32), ((3, n1, LANES), F32), a_edge, a_edge...  3.17 us
    ppermute x1, starting transfers between devices, swaps(): near = lax.ppermute(near, axis, even)  1.92 us
    pallas_call x1, Pallas kernels, body(): kernel(lambda *refs: last_kernel(aspect, *refs), [planes, ((6, n2 * LANES...  1.92 us
    ppermute x4, waiting for transfers between devices, shifts(): return (lax.ppermute(first, axis, ahead), lax.ppermute(last, axis, behind))  1.78 us
  transfers between devices with their start and end apart: 7, of which 1 were waited for; matrix products, arithmetic and copies ran while one was open for 0% of the time, Pallas kernels for 3%

profile of v2, /device:TPU:1, one launch (start us, length us, event | category | flops | bytes accessed | tf_op | source)
XLA Modules:
  0.0 65.7 jit_solution(6565303894000983341)
XLA Ops:
  0.6 3.2 %shard_map.95 = (f32[16,24,128]{2,1,0:T(8,128)}, f32[3,16,128]{2,1,0:T(8,128)}, f32[3,16,128]{2,1,0:T(8,128)}, f32[3,16,128]{2,1,0:T(8,128)}) custom-call(f32[3,128,128]{2,1,0:T(8,128)} %bitcast.9, f32[16,128]{1,0:T(8,128)} %bitcast.18, f32[16,128]{1,0:T(8,128)} %bitcast.19, f32[16,128]{1,0:T(8,128)} %bitcast.20, s32[16,128]{1,0:T(8,128)} %bitcast.16, ...), custom_call_target="tpu_custom_call" | custom-call | flops 3000000000 | tf_op jit(solution)/shard_map/pallas_call | solution.py:460
  3.8 0.0 copy-start
  3.8 0.0 copy-start.1
  3.8 0.0 copy-start.3
  3.8 0.0 copy-start.4
  3.9 17.6 %all-to-all-start = ((f32[16,24,128]{2,1,0:T(8,128)}), f32[16,24,128]{2,1,0:T(8,128)S(1)}, u32[]{:S(2)}, u32[]{:S(2)}) async-start(f32[16,24,128]{2,1,0:T(8,128)} %get-tuple-element.26), calls=%async_computation | async-start | bytes 393216 | tf_op jit(solution)/shard_map/all_to_all | solution.py:480
  21.5 0.0 copy-done
  21.5 0.0 copy-done.1
  21.5 0.0 copy-done.3
  21.5 0.0 copy-done.4
  21.5 0.0 copy-start.6
  21.5 0.8 %shard_map.96 = (f32[3,128,128]{2,1,0:T(8,128)S(1)}, f32[9,8,128]{2,1,0:T(8,128)S(1)}, f32[9,8,128]{2,1,0:T(8,128)S(1)}, s32[32,128]{1,0:T(8,128)S(1)}) custom-call(f32[3,16,128]{2,1,0:T(8,128)S(1)} %copy-done.4, s32[16,128]{1,0:T(8,128)S(1)} %bitcast.17, f32[3,128,128]{2,1,0:T(8,128)S(1)} %bitcast.10, s32[32,128]{1,0:T(8,128)S(1)} %bitcast.13), custom_call_target="tpu_custom_call" | custom-call | flops 1400000000 | tf_op jit(solution)/shard_map/pallas_call | solution.py:482
  22.3 11.0 %collective-permute-start = (f32[9,8,128]{2,1,0:T(8,128)S(1)}, f32[9,8,128]{2,1,0:T(8,128)S(1)}, u32[]{:S(2)}, u32[]{:S(2)}) collective-permute-start(f32[9,8,128]{2,1,0:T(8,128)S(1)} %get-tuple-element.22), channel_id=1, source_target_pairs={{0,1008},{16,32},{32,16},{48,64},{64,48},{80,96},{96,80},{112,128}... | collective-permute-start | bytes 110600 | tf_op jit(solution)/shard_map/ppermute | solution.py:441
  33.3 1.9 %collective-permute-start.1 = (f32[9,8,128]{2,1,0:T(8,128)S(1)}, f32[9,8,128]{2,1,0:T(8,128)S(1)}, u32[]{:S(2)}, u32[]{:S(2)}) collective-permute-start(f32[9,8,128]{2,1,0:T(8,128)S(1)} %get-tuple-element.23), channel_id=1, source_target_pairs={{0,16},{16,0},{32,48},{48,32},{64,80},{80,64},{96,112},{112,96},{1... | collective-permute-start | bytes 110600 | tf_op jit(solution)/shard_map/ppermute | solution.py:440
  35.3 0.4 collective-permute-start.2
  35.6 0.0 copy-done.5
  35.6 1.6 %collective-permute-start.3 = (f32[3,16,128]{2,1,0:T(8,128)S(1)}, f32[3,16,128]{2,1,0:T(8,128)S(1)}, u32[]{:S(2)}, u32[]{:S(2)}) collective-permute-start(f32[3,16,128]{2,1,0:T(8,128)S(1)} %copy-done.5), channel_id=1, source_target_pairs={{0,1},{1,2},{2,3},{3,4},{4,5},{5,6},{6,7},{7,8},{8,9},{9,10},{10,1... | collective-permute-start | bytes 73736 | tf_op jit(solution)/shard_map/ppermute | solution.py:433
  37.2 1.8 %collective-permute-done.2.refs_4_ = f32[3,16,128]{2,1,0:T(8,128)S(1)} collective-permute-done((f32[3,16,128]{2,1,0:T(8,128)S(1)}, f32[3,16,128]{2,1,0:T(8,128)S(1)}, u32[]{:S(2)}, u32[]{:S(2)}) %collective-permute-start.2) | collective-permute-done | bytes 24608 | tf_op jit(solution)/shard_map/ppermute | solution.py:433
  39.0 0.0 collective-permute-done.3.refs_5_
  39.0 0.0 collective-permute-done.refs_2_.refs_4_
  39.0 0.0 collective-permute-done.1.refs_3_.refs_5_
  39.0 0.0 all-to-all-done.refs_6_.arrived
  39.0 0.0 copy-start.2
  39.0 0.5 shard_map.97
  39.5 3.7 %collective-permute-start.4 = (f32[56,128]{1,0:T(8,128)S(1)}, f32[56,128]{1,0:T(8,128)S(1)}, u32[]{:S(2)}, u32[]{:S(2)}) collective-permute-start(f32[56,128]{1,0:T(8,128)S(1)} %get-tuple-element.32), channel_id=1, source_target_pairs={{1,0},{2,1},{3,2},{4,3},{5,4},{6,5},{7,6},{8,7},{9,8},{10,9},{11,1... | collective-permute-start | bytes 86024 | tf_op jit(solution)/shard_map/ppermute | solution.py:433
  43.3 0.0 collective-permute-start.5
  43.3 1.5 %shard_map.98 = (f32[3,32,128]{2,1,0:T(8,128)S(1)}, f32[8,128]{1,0:T(8,128)S(1)}) custom-call(f32[3,128,128]{2,1,0:T(8,128)S(1)} %get-tuple-element.27.middle.refs_1_, f32[2,128]{1,0:T(2,128)S(1)} %get-tuple-element.28.outer_near, s32[32,128]{1,0:T(8,128)S(1)} %bitcast.14), custom_call_target="tpu_custom_call" | custom-call | flops 1200000000 | tf_op jit(solution)/shard_map/pallas_call | solution.py:496
  44.7 0.0 collective-permute-done.4.a_next.refs_6_
  44.7 0.0 collective-permute-done.5.a_prev.refs_7_
  44.8 1.3 %shard_map.99 = (f32[16,24,128]{2,1,0:T(8,128)S(1)}, f32[3,32,128]{2,1,0:T(8,128)S(1)}) custom-call(f32[3,32,128]{2,1,0:T(8,128)S(1)} %get-tuple-element.29.gathered, f32[8,128]{1,0:T(8,128)S(1)} %get-tuple-element.30.near, f32[16,24,128]{2,1,0:T(8,128)S(1)} %all-to-all-done.refs_6_.arrived, s32[32,128]{1,0:T(8,128)S(1)} %get-tuple-element.31.slots, ...), custom_call_target="tpu_custom_call" | custom-call | flops 2400000000 | tf_op jit(solution)/shard_map/pallas_call | solution.py:499
  46.1 17.7 %all_to_all.10.refs_8_ = f32[16,24,128]{2,1,0:T(8,128)S(1)} all-to-all(f32[16,24,128]{2,1,0:T(8,128)S(1)} %get-tuple-element.35), channel_id=1, replica_groups=mesh['axial'=64,'azim'=16] {'azim'}, dimensions={0} | all-to-all | bytes 393216 | tf_op jit(solution)/shard_map/all_to_all | solution.py:506
  63.8 1.9 %shard_map.100 = (f32[3,128,128]{2,1,0:T(8,128)}, f32[6,4096]{1,0:T(8,128)}) custom-call(f32[3,128,128]{2,1,0:T(8,128)S(1)} %bitcast.12, f32[3,128,128]{2,1,0:T(8,128)S(1)} %get-tuple-element.27.middle.refs_1_, f32[3,32,128]{2,1,0:T(8,128)S(1)} %get-tuple-element.34.refs_2_, s32[32,128]{1,0:T(8,128)S(1)} %bitcast.15, ...), custom_call_target="tpu_custom_call" | custom-call | flops 1800000000 | tf_op jit(solution)/shard_map/pallas_call | solution.py:507
  (3 shorter events, 0.0 us)
Async XLA Ops:
  3.8 17.7 %copy-start = (f32[3,16,8,128]{3,2,1,0:T(8,128)S(1)}, f32[3,16,8,128]{3,2,1,0:T(8,128)}, u32[]{:S(2)}) copy-start(f32[3,16,8,128]{3,2,1,0:T(8,128)} %param.8) | copy-start | bytes 589828
  3.8 17.7 %copy-start.1 = (s32[4096,1]{0,1:T(1,128)S(1)}, s32[4096,1]{0,1:T(1,128)}, u32[]{:S(2)}) copy-start(s32[4096,1]{0,1:T(1,128)} %param.14) | copy-start | bytes 49156
  3.8 17.7 %copy-start.3 = (s32[2048]{0:T(1024)S(1)}, s32[2048]{0:T(1024)}, u32[]{:S(2)}) copy-start(s32[2048]{0:T(1024)} %param.13) | copy-start | bytes 24580
  3.8 17.6 %copy-start.4 = (f32[3,16,128]{2,1,0:T(8,128)S(1)}, f32[3,16,128]{2,1,0:T(8,128)}, u32[]{:S(2)}) copy-start(f32[3,16,128]{2,1,0:T(8,128)} %get-tuple-element.20.refs_0_) | copy-start | bytes 73732
  3.9 35.1 %all-to-all-start = ((f32[16,24,128]{2,1,0:T(8,128)}), f32[16,24,128]{2,1,0:T(8,128)S(1)}, u32[]{:S(2)}, u32[]{:S(2)}) async-start(f32[16,24,128]{2,1,0:T(8,128)} %get-tuple-element.26), calls=%async_computation | async-start | bytes 393216 | tf_op jit(solution)/shard_map/all_to_all | solution.py:480
  21.5 13.7 %copy-start.6 = (f32[3,16,128]{2,1,0:T(8,128)S(1)}, f32[3,16,128]{2,1,0:T(8,128)}, u32[]{:S(2)}) copy-start(f32[3,16,128]{2,1,0:T(8,128)} %get-tuple-element.24) | copy-start | bytes 73732
  21.5 14.1 %copy-start.5 = (f32[3,16,128]{2,1,0:T(8,128)S(1)}, f32[3,16,128]{2,1,0:T(8,128)}, u32[]{:S(2)}) copy-start(f32[3,16,128]{2,1,0:T(8,128)} %get-tuple-element.25) | copy-start | bytes 73732
  22.3 16.6 %collective-permute-start = (f32[9,8,128]{2,1,0:T(8,128)S(1)}, f32[9,8,128]{2,1,0:T(8,128)S(1)}, u32[]{:S(2)}, u32[]{:S(2)}) collective-permute-start(f32[9,8,128]{2,1,0:T(8,128)S(1)} %get-tuple-element.22), channel_id=1, source_target_pairs={{0,1008},{16,32},{32,16},{48,64},{64,48},{80,96},{96,80},{112,128}... | collective-permute-start | bytes 110600 | tf_op jit(solution)/shard_map/ppermute | solution.py:441
  33.3 5.7 %collective-permute-start.1 = (f32[9,8,128]{2,1,0:T(8,128)S(1)}, f32[9,8,128]{2,1,0:T(8,128)S(1)}, u32[]{:S(2)}, u32[]{:S(2)}) collective-permute-start(f32[9,8,128]{2,1,0:T(8,128)S(1)} %get-tuple-element.23), channel_id=1, source_target_pairs={{0,16},{16,0},{32,48},{48,32},{64,80},{80,64},{96,112},{112,96},{1... | collective-permute-start | bytes 110600 | tf_op jit(solution)/shard_map/ppermute | solution.py:440
  35.3 3.7 %collective-permute-start.2 = (f32[3,16,128]{2,1,0:T(8,128)S(1)}, f32[3,16,128]{2,1,0:T(8,128)S(1)}, u32[]{:S(2)}, u32[]{:S(2)}) collective-permute-start(f32[3,16,128]{2,1,0:T(8,128)S(1)} %copy-done.6), channel_id=1, source_target_pairs={{1,0},{2,1},{3,2},{4,3},{5,4},{6,5},{7,6},{8,7},{9,8},{10,9},{11,1... | collective-permute-start | bytes 73736 | tf_op jit(solution)/shard_map/ppermute | solution.py:433
  35.6 3.3 %collective-permute-start.3 = (f32[3,16,128]{2,1,0:T(8,128)S(1)}, f32[3,16,128]{2,1,0:T(8,128)S(1)}, u32[]{:S(2)}, u32[]{:S(2)}) collective-permute-start(f32[3,16,128]{2,1,0:T(8,128)S(1)} %copy-done.5), channel_id=1, source_target_pairs={{0,1},{1,2},{2,3},{3,4},{4,5},{5,6},{6,7},{7,8},{8,9},{9,10},{10,1... | collective-permute-start | bytes 73736 | tf_op jit(solution)/shard_map/ppermute | solution.py:433
  39.0 4.3 %copy-start.2 = (s32[4096]{0:T(1024)S(1)}, s32[4096]{0:T(1024)}, u32[]{:S(2)}) copy-start(s32[4096]{0:T(1024)} %param.15) | copy-start | bytes 49156
  39.5 5.2 %collective-permute-start.4 = (f32[56,128]{1,0:T(8,128)S(1)}, f32[56,128]{1,0:T(8,128)S(1)}, u32[]{:S(2)}, u32[]{:S(2)}) collective-permute-start(f32[56,128]{1,0:T(8,128)S(1)} %get-tuple-element.32), channel_id=1, source_target_pairs={{1,0},{2,1},{3,2},{4,3},{5,4},{6,5},{7,6},{8,7},{9,8},{10,9},{11,1... | collective-permute-start | bytes 86024 | tf_op jit(solution)/shard_map/ppermute | solution.py:433
  43.3 1.5 %collective-permute-start.5 = (f32[56,128]{1,0:T(8,128)S(1)}, f32[56,128]{1,0:T(8,128)S(1)}, u32[]{:S(2)}, u32[]{:S(2)}) collective-permute-start(f32[56,128]{1,0:T(8,128)S(1)} %get-tuple-element.33), channel_id=1, source_target_pairs={{0,1},{1,2},{2,3},{3,4},{4,5},{5,6},{6,7},{7,8},{8,9},{9,10},{10,1... | collective-permute-start | bytes 86024 | tf_op jit(solution)/shard_map/ppermute | solution.py:433

commit v3 on v2

--- a/solution.py
+++ b/solution.py
@@ -158,7 +158,7 @@
 
 def send_near(out_ref, near):
     for t in range(out_ref.shape[0]):
-        out_ref[t, 2 * SUB :, :] = near
+        out_ref[t, 2 * SUB : 3 * SUB, :] = near
 
 
 def columns_of(ref, c, at, count_z, count_a):
@@ -167,12 +167,10 @@
 
 def first_kernel(
     gas_hbm, mass_hbm, temp_hbm, speed_hbm, cell_hbm, dest_hbm,
-    out, source, first_a, last_a,
+    out, source,
     gas, mass, temp, speed, cell, dest, sems, gathered, slots, records,
 ):
     sectors = out.shape[0]
-    count_z = first_a.shape[1]
-    count_a = gas.shape[1] // count_z
     loads = [
         pltpu.make_async_copy(a, b, sems.at[i])
         for i, (a, b) in enumerate(
@@ -205,12 +203,9 @@
         records[pl.ds(c, n, stride=SUB), :] = states[c] + DT_STEP * change[c]
         records[pl.ds(3 + c, n, stride=SUB), :] = states[c]
     place(records, slots, out)
-    for c in range(3):
-        first_a[c] = columns_of(gas, c, 0, count_z, count_a)
-        last_a[c] = columns_of(gas, c, count_a - 1, count_z, count_a)
-
-
-def first_deposit_kernel(sectors, count_a, source, cell, gas, dest, out, far_z, near_z, slots):
+
+
+def first_deposit_kernel(sectors, count_a, source, cell, gas, dest, out, far_z, near_z, first_a, last_a, slots):
     total = deposit(source, cell, out.shape[1], out.shape[2])
     end = out.shape[1]
     even = (lax.axis_index("axial") & 1) == 0
@@ -225,17 +220,27 @@
         for i in range(3):
             near_z[3 * c + i] = jnp.where(even, last[i], first[i])
             far_z[3 * c + i] = jnp.where(even, first[i], last[i])
+    count_z = first_a.shape[1]
+    for c in range(3):
+        for edge, at, inner in ((first_a, 0, 1), (last_a, count_a - 1, count_a - 2)):
+            edge[3 * c] = columns_of(gas, c, at, count_z, count_a)
+            edge[3 * c + 1] = columns_of(gas, c, inner, count_z, count_a)
+            edge[3 * c + 2] = columns_of(out, c, at, count_z, count_a)
     slots[...] = slot_of(dest[...], sectors, 2 * LANES)
 
 
-def stencil(fields, following, preceding, right_edge, left_edge, near, added, aspect):
+def last_deposit_kernel(source, cell, out):
+    total = deposit(source, cell, out.shape[1], out.shape[2])
+    for c in range(3):
+        out[c] = total[c]
+
+
+def stencil(fields, following, preceding, right, left, near, added, aspect):
     shape = fields[0].shape
-    count_a = shape[1]
     pos = iota((1, 1, LANES), 2).astype(F32) + 0.5
     inverse = 1.0 / (12.0 * pos)
     geometry = aspect * aspect / jnp.maximum(pos / LANES, RADIUS_FLOOR) ** 2
     lane = iota(shape, 2)
-    column = iota(shape, 1)
     results = []
     for c in range(3):
         q = fields[c]
@@ -251,11 +256,9 @@
         )
         minus_one = jnp.where(lane == 0, near_0, down)
         minus_two = jnp.where(lane == 0, near_1, jnp.where(lane == 1, near_0, down_2))
-        right = jnp.where(column == count_a - 1, right_edge[c], pltpu.roll(q, count_a - 1, 1))
-        left = jnp.where(column == 0, left_edge[c], pltpu.roll(q, 1, 1))
         laplace = (16.0 * (plus_one + minus_one) - 30.0 * q - plus_two - minus_two) / 12.0
         laplace = laplace + (8.0 * (plus_one - minus_one) - plus_two + minus_two) * inverse
-        laplace = laplace + geometry * (right + left - 2.0 * q)
+        laplace = laplace + geometry * (right[c] + left[c] - 2.0 * q)
         laplace = laplace + (following[c] + preceding[c] - 2.0 * q) / 16.0
         results.append(
             q
@@ -266,6 +269,19 @@
     return results
 
 
+def sides(fields, right_edge, left_edge):
+    count_a = fields[0].shape[1]
+    column = iota(fields[0].shape, 1)
+    pairs = [
+        (
+            jnp.where(column == count_a - 1, right_edge[c], pltpu.roll(q, count_a - 1, 1)),
+            jnp.where(column == 0, left_edge[c], pltpu.roll(q, 1, 1)),
+        )
+        for c, q in enumerate(fields)
+    ]
+    return [p[0] for p in pairs], [p[1] for p in pairs]
+
+
 def between(q, z_prev, z_next):
     return (
         jnp.concatenate([q[1:], z_next[None]], axis=0),
@@ -298,51 +314,45 @@
 
 
 def middle_kernel(
-    aspect, gas, added, far_z, near_z, a_next, a_prev, arrived,
-    middle, near, first_a, last_a,
+    aspect, gas, added, far_z, near_z, a_next, a_prev, arrived, cell, slots,
+    middle, out, source, gathered, records,
 ):
     count_z, count_a = a_next.shape[1], near_z.shape[1]
     shape = (count_z, count_a, LANES)
+    sectors = arrived.shape[0]
     z_next, z_prev = outer_planes(near_z, far_z)
-    across = near_columns(arrived[across_axis(arrived.shape[0]), 2 * SUB :, :])
+    across = near_columns(arrived[across_axis(sectors), 2 * SUB :, :])
     fields = [gas[c].reshape(shape) for c in range(3)]
     pairs = [between(fields[c], z_prev[3 * c], z_next[3 * c]) for c in range(3)]
     results = stencil(
         fields,
         [p[0] for p in pairs],
         [p[1] for p in pairs],
-        [a_next[c].reshape(count_z, 1, LANES) for c in range(3)],
-        [a_prev[c].reshape(count_z, 1, LANES) for c in range(3)],
+        *sides(
+            fields,
+            [a_next[3 * c].reshape(count_z, 1, LANES) for c in range(3)],
+            [a_prev[3 * c].reshape(count_z, 1, LANES) for c in range(3)],
+        ),
         column_blocks(across, count_z, count_a),
         [added[c].reshape(shape) for c in range(3)],
         aspect,
     )
     for c in range(3):
         middle[c] = results[c].reshape(middle.shape[1:])
-    outer = [planes[3 * c] for c in range(3) for planes in (z_prev, z_next)]
-    for i, plane in enumerate(outer):
-        first_a[3 * count_z + i] = plane[0]
-        last_a[3 * count_z + i] = plane[count_a - 1]
-    for c in range(3):
-        first_a[c * count_z : (c + 1) * count_z] = columns_of(middle, c, 0, count_z, count_a)
-        last_a[c * count_z : (c + 1) * count_z] = columns_of(middle, c, count_a - 1, count_z, count_a)
-    unused = first_a.shape[0] - 3 * count_z - len(outer)
-    first_a[3 * count_z + len(outer) :] = jnp.zeros((unused, LANES), F32)
-    last_a[3 * count_z + len(outer) :] = jnp.zeros((unused, LANES), F32)
-    rest = jnp.zeros((LANES - len(outer) * count_a, LANES), F32)
-    near[...] = jnp.concatenate(outer + [rest], axis=0).T[:2]
-
-
-def sample_kernel(middle, outer_near, cell, gathered, near):
     table, turned = gas_table([middle[c] for c in range(3)])
     sample(table, cell, gathered)
-    near[...] = jnp.concatenate([t[:2] for t in turned] + [outer_near[...]], axis=0)
-
-
-def second_kernel(gathered, near, arrived, slots, a_next, a_prev, out, source, records):
-    del a_next, a_prev
-    send_near(out, near[...])
-    sectors = arrived.shape[0]
+
+    outer = [planes[3 * c] for c in range(3) for planes in (z_prev, z_next)]
+    rest = jnp.zeros((LANES - len(outer) * count_a, LANES), F32)
+    outer_near = jnp.concatenate(outer + [rest], axis=0).T[:2]
+    near = jnp.concatenate([t[:2] for t in turned] + [outer_near], axis=0)
+    spare = jnp.zeros((SUB - len(outer), LANES), F32)
+    to_right = jnp.concatenate([p[count_a - 1 :] for p in outer] + [spare], axis=0)
+    to_left = jnp.concatenate([p[:1] for p in outer] + [spare], axis=0)
+    right, across_to = neighbour(1, sectors), across_axis(sectors)
+    for t in range(sectors):
+        out[t, 2 * SUB :, :] = jnp.where(across_to == t, near, jnp.where(right == t, to_right, to_left))
+
     for half in range(2):
         values = [arrived[:, half * SUB + c, :] for c in range(6)]
         now, anchor = values[:3], values[3:]
@@ -359,28 +369,38 @@
     place(records, slots, out)
 
 
-def last_kernel(aspect, gas, middle, source, cell, far_z, near_z, a_next, a_prev, arrived, out, records):
-    added = deposit(source, cell, gas.shape[1], gas.shape[2])
+def neighbour(step, sectors):
+    return (lax.axis_index("azim") + step + sectors) % sectors
+
+
+def last_kernel(
+    aspect, gas, middle, added, far_z, near_z, a_next, a_prev, earlier, arrived,
+    out, records, turned_near,
+):
     count_a = near_z.shape[1]
-    z_next, z_prev = outer_planes(near_z, far_z)
     count_z = gas.shape[1] // count_a
+    sectors = arrived.shape[0]
     shape = (count_z, count_a, LANES)
     end = gas.shape[1]
-    across = near_columns(arrived[across_axis(arrived.shape[0]), 2 * SUB :, :])
-    own = count_z * 3
-
-    def outer(before, after):
+    z_next, z_prev = outer_planes(near_z, far_z)
+    across = near_columns(arrived[across_axis(sectors), 2 * SUB :, :])
+    ahead, behind = neighbour(1, sectors), neighbour(-1, sectors)
+    corner_next = arrived[ahead, 2 * SUB :, :]
+    corner_prev = arrived[behind, 2 * SUB :, :]
+
+    def both(before, after):
         return jnp.concatenate([before[None], after[None]], axis=0)
 
-    def outer_rows(ref, c):
-        return ref[own + 2 * c : own + 2 * c + 2, :].reshape(2, 1, LANES)
-
-    halo = stencil(
-        [outer(z_prev[3 * c], z_next[3 * c]) for c in range(3)],
-        [outer(gas[c, :count_a, :], z_next[3 * c + 1]) for c in range(3)],
-        [outer(z_prev[3 * c + 1], gas[c, end - count_a :, :]) for c in range(3)],
-        [outer_rows(a_next, c) for c in range(3)],
-        [outer_rows(a_prev, c) for c in range(3)],
+    outer = [both(z_prev[3 * c], z_next[3 * c]) for c in range(3)]
+    planes = stencil(
+        outer,
+        [both(gas[c, :count_a, :], z_next[3 * c + 1]) for c in range(3)],
+        [both(z_prev[3 * c + 1], gas[c, end - count_a :, :]) for c in range(3)],
+        *sides(
+            outer,
+            [corner_next[2 * c : 2 * c + 2].reshape(2, 1, LANES) for c in range(3)],
+            [corner_prev[2 * c : 2 * c + 2].reshape(2, 1, LANES) for c in range(3)],
+        ),
         [
             [
                 across[2 * c * count_a : 2 * (c + 1) * count_a, 6 + i : 7 + i].reshape(2, count_a, 1)
@@ -388,24 +408,56 @@
             ]
             for c in range(3)
         ],
-        [outer(z_prev[3 * c + 2], z_next[3 * c + 2]) for c in range(3)],
+        [both(z_prev[3 * c + 2], z_next[3 * c + 2]) for c in range(3)],
         aspect,
     )
+    columns = []
+    for edge, corner, sector, at in (
+        (a_prev, corner_prev, behind, count_a - 1),
+        (a_next, corner_next, ahead, 0),
+    ):
+        turned_near[...] = near_columns(earlier[sector ^ (sectors // 2), 2 * SUB :, :])
+        near = turned_near[pl.ds(at, count_z, stride=count_a), :]
+        own = [columns_of(gas, c, count_a - 1 - at, count_z, count_a) for c in range(3)]
+        inner = [edge[3 * c + 1] for c in range(3)]
+        fields = [edge[3 * c] for c in range(3)]
+        following = [
+            jnp.concatenate([fields[c][1:], corner[2 * c + 1 : 2 * c + 2]], axis=0) for c in range(3)
+        ]
+        preceding = [
+            jnp.concatenate([corner[2 * c : 2 * c + 1], fields[c][:-1]], axis=0) for c in range(3)
+        ]
+        columns.append(
+            stencil(
+                [f[None] for f in fields],
+                [f[None] for f in following],
+                [f[None] for f in preceding],
+                [f[None] for f in own],
+                [f[None] for f in inner],
+                [[near[None, :, 2 * c + i : 2 * c + i + 1] for i in range(2)] for c in range(3)],
+                [edge[3 * c + 2][None] for c in range(3)],
+                aspect,
+            )
+        )
+    left, right = columns
     fields = [middle[c].reshape(shape) for c in range(3)]
-    pairs = [between(fields[c], halo[c][0], halo[c][1]) for c in range(3)]
+    pairs = [between(fields[c], planes[c][0], planes[c][1]) for c in range(3)]
     results = stencil(
         fields,
         [p[0] for p in pairs],
         [p[1] for p in pairs],
-        [a_next[c * count_z : (c + 1) * count_z, :].reshape(count_z, 1, LANES) for c in range(3)],
-        [a_prev[c * count_z : (c + 1) * count_z, :].reshape(count_z, 1, LANES) for c in range(3)],
+        *sides(
+            fields,
+            [right[c].reshape(count_z, 1, LANES) for c in range(3)],
+            [left[c].reshape(count_z, 1, LANES) for c in range(3)],
+        ),
         column_blocks(across, count_z, count_a),
         [added[c].reshape(shape) for c in range(3)],
         aspect,
     )
     for c in range(3):
         out[c] = 0.75 * gas[c] + 0.25 * results[c].reshape(out.shape[1:])
-    for s in range(arrived.shape[0]):
+    for s in range(sectors):
         for half in range(2):
             at = (2 * s + half) * LANES
             records[:, at : at + LANES] = arrived[s, half * SUB : half * SUB + 6, :]
@@ -451,15 +503,14 @@
     gas = gas_fields.reshape(3, cells, radial)
     block = (sectors, 3 * SUB, LANES)
     z_edge = ((9, count_a, radial), F32)
-    a_edge = ((3, count_z, radial), F32)
-    a_edge_2 = ((-(-(3 * count_z + 6) // SUB) * SUB, radial), F32)
+    a_edge = ((9, count_z, radial), F32)
     planes = ((3, cells, radial), F32)
     cell_1 = cell_first.reshape(n1, LANES)
     cell_2 = cell_second.reshape(n2, LANES)
 
-    out_1, source_1, first_a, last_a = kernel(
+    out_1, source_1 = kernel(
         first_kernel,
-        [(block, F32), ((3, n1, LANES), F32), a_edge, a_edge],
+        [(block, F32), ((3, n1, LANES), F32)],
         [pltpu.VMEM((3, cells, radial), F32)]
         + [pltpu.VMEM((n1, LANES), F32)] * 3
         + [pltpu.VMEM((n1, LANES), jnp.int32)] * 2
@@ -478,38 +529,31 @@
         dest_first.reshape(n1, LANES),
     )
     arrived_1 = lax.all_to_all(out_1, "azim", split_axis=0, concat_axis=0, tiled=True)
-    a_next, a_prev = shifts(first_a, last_a, "azim")
-    added_1, far_z, near_z, slots_2 = kernel(
+    added_1, far_z, near_z, first_a, last_a, slots_2 = kernel(
         lambda *refs: first_deposit_kernel(sectors, count_a, *refs),
-        [planes, z_edge, z_edge, ((n2, LANES), jnp.int32)],
+        [planes, z_edge, z_edge, a_edge, a_edge, ((n2, LANES), jnp.int32)],
         n_in=4,
         cost=1.4,
     )(source_1, cell_1, gas, dest_second.reshape(n2, LANES))
     far_z, near_z = swaps(near_z, far_z, "axial")
-
-    middle, outer_near, first_a, last_a = kernel(
+    a_next, a_prev = shifts(first_a, last_a, "azim")
+
+    middle, out_2, source_2 = kernel(
         lambda *refs: middle_kernel(aspect, *refs),
-        [planes, ((2, LANES), F32), a_edge_2, a_edge_2],
-        n_in=7,
-    )(gas, added_1, far_z, near_z, a_next, a_prev, arrived_1)
-    a_next, a_prev = shifts(first_a, last_a, "azim")
-    gathered_2, near_2 = kernel(
-        sample_kernel, [((3, n2, LANES), F32), ((SUB, LANES), F32)], n_in=3, cost=1.2
-    )(middle, outer_near, cell_2)
-    out_2, source_2 = kernel(
-        second_kernel,
-        [(block, F32), ((3, n2, LANES), F32)],
-        [pltpu.VMEM((n2 * SUB, LANES), F32)],
-        n_in=6,
-        cost=2.4,
-    )(gathered_2, near_2, arrived_1, slots_2, a_next, a_prev)
+        [planes, (block, F32), ((3, n2, LANES), F32)],
+        [pltpu.VMEM((3, n2, LANES), F32), pltpu.VMEM((n2 * SUB, LANES), F32)],
+        n_in=9,
+        cost=4.0,
+    )(gas, added_1, far_z, near_z, a_next, a_prev, arrived_1, cell_2, slots_2)
     arrived_2 = lax.all_to_all(out_2, "azim", split_axis=0, concat_axis=0, tiled=True)
+    (added_2,) = kernel(last_deposit_kernel, [planes], n_in=2)(source_2, cell_2)
     gas_next, drop_records = kernel(
         lambda *refs: last_kernel(aspect, *refs),
         [planes, ((6, n2 * LANES), F32)],
+        [pltpu.VMEM((LANES, LANES), F32)],
         n_in=9,
         cost=1.8,
-    )(gas, middle, source_2, cell_2, far_z, near_z, a_next, a_prev, arrived_2)
+    )(gas, middle, added_2, far_z, near_z, a_next, a_prev, arrived_1, arrived_2)
     return gas_next.reshape(gas_fields.shape), drop_records
 
 

time: 66.1 us -> 63.6 us (0.962)
  blocking collectives: 17.7 us -> 0 us
  waiting for transfers between devices: 1.79 us -> 12 us
  starting transfers between devices: 36.2 us -> 39.9 us
  Pallas kernels: 9.22 us -> 10.5 us
    all_to_all x1 -> x0, blocking collectives: 17.7 us -> none  [body(): lax.all_to_all(out_2, 'azim', split_axis=0, concat_axis=0, tiled=True)]
    all_to_all x0 -> x1, waiting for transfers between devices: none -> 9.23 us  [body(): lax.all_to_all(out_2, 'azim', split_axis=0, concat_axis=0, tiled=True)]
    all_to_all x0 -> x1, starting transfers between devices: none -> 7.67 us  [body(): lax.all_to_all(out_2, 'azim', split_axis=0, concat_axis=0, tiled=True)]
    ppermute x4 -> x2, starting transfers between devices: 5.68 us -> 1.75 us  [shifts(): return (lax.ppermute(first, axis, ahead), lax.ppermute(last, axis, behind))]
    ppermute x1, waiting for transfers between devices: 0.01 us -> 2.76 us  [swaps(): near = lax.ppermute(near, axis, even)]
    ppermute x4 -> x2, waiting for transfers between devices: 1.78 us -> 0.01 us  [shifts(): return (lax.ppermute(first, axis, ahead), lax.ppermute(last, axis, behind))]
    pallas_call x4 -> x3, Pallas kernels: 6.49 us -> 8.2 us  [the longest x1 3.94 us: body(): kernel(lambda *refs: middle_kernel(aspect, *refs), [planes, (block, F32),...]
  transfers between devices with their start and end apart: 7 -> 6, of which waited for: 1 -> 2; matrix products, arithmetic and copies ran while one was open for 0% -> 0% of each run, Pallas kernels for 3% -> 3%
where the time goes in v3:
time: 63.6 us; the launch traced here: 63.2 us
  starting transfers between devices  39.9 us (63%)
  waiting for transfers between devices  12 us (19%)
  Pallas kernels  10.5 us (17%)
  between operations  0.75 us (1%)
    all_to_all x1, starting transfers between devices, body(): lax.all_to_all(out_1, 'azim', split_axis=0, concat_axis=0, tiled=True)  17.6 us
    ppermute x1, starting transfers between devices, swaps(): return (lax.ppermute(far, axis, odd), near)  10.9 us
    all_to_all x1, waiting for transfers between devices, body(): lax.all_to_all(out_2, 'azim', split_axis=0, concat_axis=0, tiled=True)  9.23 us
    all_to_all x1, starting transfers between devices, body(): lax.all_to_all(out_2, 'azim', split_axis=0, concat_axis=0, tiled=True)  7.67 us
    pallas_call x1, Pallas kernels, body(): kernel(lambda *refs: middle_kernel(aspect, *refs), [planes, (block, F32),...  3.94 us
    pallas_call x1, Pallas kernels, body(): kernel(first_kernel, [(block, F32), ((3, n1, LANES), F32)], [pltpu.VMEM((...  3.17 us
    ppermute x1, waiting for transfers between devices, swaps(): near = lax.ppermute(near, axis, even)  2.76 us
    ppermute x1, starting transfers between devices, swaps(): near = lax.ppermute(near, axis, even)  1.92 us
  transfers between devices with their start and end apart: 6, of which 2 were waited for; matrix products, arithmetic and copies ran while one was open for 0% of the time, Pallas kernels for 3%

profile of v3, /device:TPU:1, one launch (start us, length us, event | category | flops | bytes accessed | tf_op | source)
XLA Modules:
  0.0 63.2 jit_solution(11640166663924241106)
XLA Ops:
  0.6 3.2 %shard_map.95 = (f32[16,24,128]{2,1,0:T(8,128)}, f32[3,16,128]{2,1,0:T(8,128)}) custom-call(f32[3,128,128]{2,1,0:T(8,128)} %bitcast.9, f32[16,128]{1,0:T(8,128)} %bitcast.18, f32[16,128]{1,0:T(8,128)} %bitcast.19, f32[16,128]{1,0:T(8,128)} %bitcast.20, s32[16,128]{1,0:T(8,128)} %bitcast.16, s32[16,128]{1,0:T(8,128)} %bitcast.21), custom_call_target="tpu_custom_call" | custom-call | flops 3000000000 | tf_op jit(solution)/shard_map/pallas_call | solution.py:511
  3.8 0.0 copy-start
  3.8 0.0 copy-start.1
  3.8 0.0 copy-start.3
  3.8 0.0 copy-start.4
  3.9 17.6 %all-to-all-start = ((f32[16,24,128]{2,1,0:T(8,128)}), f32[16,24,128]{2,1,0:T(8,128)S(1)}, u32[]{:S(2)}, u32[]{:S(2)}) async-start(f32[16,24,128]{2,1,0:T(8,128)} %get-tuple-element.21), calls=%async_computation | async-start | bytes 393216 | tf_op jit(solution)/shard_map/all_to_all | solution.py:531
  21.5 0.0 copy-done
  21.5 0.0 copy-done.1
  21.5 0.0 copy-done.3
  21.5 0.0 copy-done.4
  21.5 0.0 copy-start.2
  21.5 0.8 %shard_map.96 = (f32[3,128,128]{2,1,0:T(8,128)S(1)}, f32[9,8,128]{2,1,0:T(8,128)S(1)}, f32[9,8,128]{2,1,0:T(8,128)S(1)}, f32[9,16,128]{2,1,0:T(8,128)S(1)}, f32[...) custom-call(f32[3,16,128]{2,1,0:T(8,128)S(1)} %copy-done.4, s32[16,128]{1,0:T(8,128)S(1)} %bitcast.17, ...), custom_call_target="tpu_custom_call" | custom-call | flops 1400000000 | tf_op jit(solution)/shard_map/pallas_call | solution.py:532
  22.3 0.2 collective-permute-start.2
  22.6 1.5 %collective-permute-start.3 = (f32[9,16,128]{2,1,0:T(8,128)S(1)}, f32[9,16,128]{2,1,0:T(8,128)S(1)}, u32[]{:S(2)}, u32[]{:S(2)}) collective-permute-start(f32[9,16,128]{2,1,0:T(8,128)S(1)} %get-tuple-element.20), channel_id=1, source_target_pairs={{0,1},{1,2},{2,3},{3,4},{4,5},{5,6},{6,7},{7,8},{8,9},{9,10},{10,1... | collective-permute-start | bytes 221192 | tf_op jit(solution)/shard_map/ppermute | solution.py:485
  24.1 10.9 %collective-permute-start = (f32[9,8,128]{2,1,0:T(8,128)S(1)}, f32[9,8,128]{2,1,0:T(8,128)S(1)}, u32[]{:S(2)}, u32[]{:S(2)}) collective-permute-start(f32[9,8,128]{2,1,0:T(8,128)S(1)} %get-tuple-element.17), channel_id=1, source_target_pairs={{0,1008},{16,32},{32,16},{48,64},{64,48},{80,96},{96,80},{112,128}... | collective-permute-start | bytes 110600 | tf_op jit(solution)/shard_map/ppermute | solution.py:493
  35.0 1.9 %collective-permute-start.1 = (f32[9,8,128]{2,1,0:T(8,128)S(1)}, f32[9,8,128]{2,1,0:T(8,128)S(1)}, u32[]{:S(2)}, u32[]{:S(2)}) collective-permute-start(f32[9,8,128]{2,1,0:T(8,128)S(1)} %get-tuple-element.18), channel_id=1, source_target_pairs={{0,16},{16,0},{32,48},{48,32},{64,80},{80,64},{96,112},{112,96},{1... | collective-permute-start | bytes 110600 | tf_op jit(solution)/shard_map/ppermute | solution.py:492
  37.0 0.0 collective-permute-done.refs_2_.refs_3_
  37.0 2.8 %collective-permute-done.1.refs_3_.refs_4_ = f32[9,8,128]{2,1,0:T(8,128)S(1)} collective-permute-done((f32[9,8,128]{2,1,0:T(8,128)S(1)}, f32[9,8,128]{2,1,0:T(8,128)S(1)}, u32[]{:S(2)}, u32[]{:S(2)}) %collective-permute-start.1) | collective-permute-done | bytes 36896 | tf_op jit(solution)/shard_map/ppermute | solution.py:492
  39.7 0.0 collective-permute-done.2.refs_4_.refs_5_
  39.7 0.0 collective-permute-done.3.refs_5_.refs_6_
  39.8 0.0 all-to-all-done.refs_6_.refs_7_
  39.8 0.0 copy-done.2
  39.8 3.9 %shard_map.97 = (f32[3,128,128]{2,1,0:T(8,128)S(1)}, f32[16,24,128]{2,1,0:T(8,128)}, f32[3,32,128]{2,1,0:T(8,128)S(1)}) custom-call(f32[3,128,128]{2,1,0:T(8,128)S(1)} %bitcast.11, f32[3,128,128]{2,1,0:T(8,128)S(1)} %get-tuple-element.16.refs_1_, f32[9,8,128]{2,1,0:T(8,128)S(1)} %collective-permute-done.refs_2_.refs_3_, ...), custom_call_target="tpu_custom_call" | custom-call | flops 4000000000 | tf_op jit(solution)/shard_map/pallas_call | solution.py:541
  43.7 7.7 %all-to-all-start.1 = ((f32[16,24,128]{2,1,0:T(8,128)}), f32[16,24,128]{2,1,0:T(8,128)S(1)}, u32[]{:S(2)}, u32[]{:S(2)}) async-start(f32[16,24,128]{2,1,0:T(8,128)} %get-tuple-element.25), calls=%async_computation.1 | async-start | bytes 393216 | tf_op jit(solution)/shard_map/all_to_all | solution.py:548
  51.4 1.1 %shard_map.98.refs_2_ = f32[3,128,128]{2,1,0:T(8,128)S(1)} custom-call(f32[3,32,128]{2,1,0:T(8,128)S(1)} %get-tuple-element.24.source, s32[32,128]{1,0:T(8,128)S(1)} %bitcast.15), custom_call_target="tpu_custom_call" | custom-call | flops 1000000000 | tf_op jit(solution)/shard_map/pallas_call | solution.py:549
  52.5 9.2 %all-to-all-done.1.refs_8_ = f32[16,24,128]{2,1,0:T(8,128)S(1)} async-done(((f32[16,24,128]{2,1,0:T(8,128)}), f32[16,24,128]{2,1,0:T(8,128)S(1)}, u32[]{:S(2)}, u32[]{:S(2)}) %all-to-all-start.1) | async-done | bytes 196640 | tf_op jit(solution)/shard_map/all_to_all | solution.py:548
  61.7 1.5 %shard_map.99 = (f32[3,128,128]{2,1,0:T(8,128)}, f32[6,4096]{1,0:T(8,128)}) custom-call(f32[3,128,128]{2,1,0:T(8,128)S(1)} %bitcast.12, f32[3,128,128]{2,1,0:T(8,128)S(1)} %get-tuple-element.23.refs_1_, f32[3,128,128]{2,1,0:T(8,128)S(1)} %shard_map.98.refs_2_, f32[9,8,128]{2,1,0:T(8,128)S(1)} %collective-permute-done.refs_2_.refs_3_, ...), custom_call_target="tpu_custom_call" | custom-call | flops 1800000000 | tf_op jit(solution)/shard_map/pallas_call | solution.py:550
Async XLA Ops:
  3.8 17.7 %copy-start = (f32[3,16,8,128]{3,2,1,0:T(8,128)S(1)}, f32[3,16,8,128]{3,2,1,0:T(8,128)}, u32[]{:S(2)}) copy-start(f32[3,16,8,128]{3,2,1,0:T(8,128)} %param.8) | copy-start | bytes 589828
  3.8 17.7 %copy-start.1 = (s32[4096,1]{0,1:T(1,128)S(1)}, s32[4096,1]{0,1:T(1,128)}, u32[]{:S(2)}) copy-start(s32[4096,1]{0,1:T(1,128)} %param.14) | copy-start | bytes 49156
  3.8 17.6 %copy-start.3 = (s32[2048]{0:T(1024)S(1)}, s32[2048]{0:T(1024)}, u32[]{:S(2)}) copy-start(s32[2048]{0:T(1024)} %param.13) | copy-start | bytes 24580
  3.8 17.6 %copy-start.4 = (f32[3,16,128]{2,1,0:T(8,128)S(1)}, f32[3,16,128]{2,1,0:T(8,128)}, u32[]{:S(2)}) copy-start(f32[3,16,128]{2,1,0:T(8,128)} %get-tuple-element.15.refs_0_) | copy-start | bytes 73732
  3.9 35.9 %all-to-all-start = ((f32[16,24,128]{2,1,0:T(8,128)}), f32[16,24,128]{2,1,0:T(8,128)S(1)}, u32[]{:S(2)}, u32[]{:S(2)}) async-start(f32[16,24,128]{2,1,0:T(8,128)} %get-tuple-element.21), calls=%async_computation | async-start | bytes 393216 | tf_op jit(solution)/shard_map/all_to_all | solution.py:531
  21.5 18.3 %copy-start.2 = (s32[4096]{0:T(1024)S(1)}, s32[4096]{0:T(1024)}, u32[]{:S(2)}) copy-start(s32[4096]{0:T(1024)} %param.15) | copy-start | bytes 49156
  22.3 17.4 %collective-permute-start.2 = (f32[9,16,128]{2,1,0:T(8,128)S(1)}, f32[9,16,128]{2,1,0:T(8,128)S(1)}, u32[]{:S(2)}, u32[]{:S(2)}) collective-permute-start(f32[9,16,128]{2,1,0:T(8,128)S(1)} %get-tuple-element.19), channel_id=1, source_target_pairs={{1,0},{2,1},{3,2},{4,3},{5,4},{6,5},{7,6},{8,7},{9,8},{10,9},{11,1... | collective-permute-start | bytes 221192 | tf_op jit(solution)/shard_map/ppermute | solution.py:485
  22.6 17.2 %collective-permute-start.3 = (f32[9,16,128]{2,1,0:T(8,128)S(1)}, f32[9,16,128]{2,1,0:T(8,128)S(1)}, u32[]{:S(2)}, u32[]{:S(2)}) collective-permute-start(f32[9,16,128]{2,1,0:T(8,128)S(1)} %get-tuple-element.20), channel_id=1, source_target_pairs={{0,1},{1,2},{2,3},{3,4},{4,5},{5,6},{6,7},{7,8},{8,9},{9,10},{10,1... | collective-permute-start | bytes 221192 | tf_op jit(solution)/shard_map/ppermute | solution.py:485
  24.1 12.9 %collective-permute-start = (f32[9,8,128]{2,1,0:T(8,128)S(1)}, f32[9,8,128]{2,1,0:T(8,128)S(1)}, u32[]{:S(2)}, u32[]{:S(2)}) collective-permute-start(f32[9,8,128]{2,1,0:T(8,128)S(1)} %get-tuple-element.17), channel_id=1, source_target_pairs={{0,1008},{16,32},{32,16},{48,64},{64,48},{80,96},{96,80},{112,128}... | collective-permute-start | bytes 110600 | tf_op jit(solution)/shard_map/ppermute | solution.py:493
  35.0 4.7 %collective-permute-start.1 = (f32[9,8,128]{2,1,0:T(8,128)S(1)}, f32[9,8,128]{2,1,0:T(8,128)S(1)}, u32[]{:S(2)}, u32[]{:S(2)}) collective-permute-start(f32[9,8,128]{2,1,0:T(8,128)S(1)} %get-tuple-element.18), channel_id=1, source_target_pairs={{0,16},{16,0},{32,48},{48,32},{64,80},{80,64},{96,112},{112,96},{1... | collective-permute-start | bytes 110600 | tf_op jit(solution)/shard_map/ppermute | solution.py:492
  43.7 18.0 %all-to-all-start.1 = ((f32[16,24,128]{2,1,0:T(8,128)}), f32[16,24,128]{2,1,0:T(8,128)S(1)}, u32[]{:S(2)}, u32[]{:S(2)}) async-start(f32[16,24,128]{2,1,0:T(8,128)} %get-tuple-element.25), calls=%async_computation.1 | async-start | bytes 393216 | tf_op jit(solution)/shard_map/all_to_all | solution.py:548

commit v4 on v3

--- a/solution.py
+++ b/solution.py
@@ -205,7 +205,7 @@
     place(records, slots, out)
 
 
-def first_deposit_kernel(sectors, count_a, source, cell, gas, dest, out, far_z, near_z, first_a, last_a, slots):
+def first_deposit_kernel(count_a, source, cell, gas, out, far_z, near_z, first_a, last_a):
     total = deposit(source, cell, out.shape[1], out.shape[2])
     end = out.shape[1]
     even = (lax.axis_index("axial") & 1) == 0
@@ -226,6 +226,10 @@
             edge[3 * c] = columns_of(gas, c, at, count_z, count_a)
             edge[3 * c + 1] = columns_of(gas, c, inner, count_z, count_a)
             edge[3 * c + 2] = columns_of(out, c, at, count_z, count_a)
+
+
+def slot_kernel(sectors, dest, after, slots):
+    del after
     slots[...] = slot_of(dest[...], sectors, 2 * LANES)
 
 
@@ -529,12 +533,15 @@
         dest_first.reshape(n1, LANES),
     )
     arrived_1 = lax.all_to_all(out_1, "azim", split_axis=0, concat_axis=0, tiled=True)
-    added_1, far_z, near_z, first_a, last_a, slots_2 = kernel(
-        lambda *refs: first_deposit_kernel(sectors, count_a, *refs),
-        [planes, z_edge, z_edge, a_edge, a_edge, ((n2, LANES), jnp.int32)],
-        n_in=4,
+    added_1, far_z, near_z, first_a, last_a = kernel(
+        lambda *refs: first_deposit_kernel(count_a, *refs),
+        [planes, z_edge, z_edge, a_edge, a_edge],
+        n_in=3,
         cost=1.4,
-    )(source_1, cell_1, gas, dest_second.reshape(n2, LANES))
+    )(source_1, cell_1, gas)
+    (slots_2,) = kernel(
+        lambda *refs: slot_kernel(sectors, *refs), [((n2, LANES), jnp.int32)], n_in=2
+    )(dest_second.reshape(n2, LANES), added_1)
     far_z, near_z = swaps(near_z, far_z, "axial")
     a_next, a_prev = shifts(first_a, last_a, "azim")
 

time: 63.6 us -> 63.8 us (level)
  waiting for transfers between devices: 12 us -> 10.8 us
  starting transfers between devices: 39.9 us -> 41 us
    ppermute x1, waiting for transfers between devices: 2.76 us -> 0.45 us  [swaps(): near = lax.ppermute(near, axis, even)]
    ppermute x2, waiting for transfers between devices: 0.01 us -> 1.16 us  [shifts(): return (lax.ppermute(first, axis, ahead), lax.ppermute(last, axis, behind))]
    all_to_all x1, starting transfers between devices: 7.67 us -> 8.57 us  [body(): lax.all_to_all(out_2, 'azim', split_axis=0, concat_axis=0, tiled=True)]
  transfers between devices with their start and end apart: 6 -> 6, of which waited for: 2 -> 3; matrix products, arithmetic and copies ran while one was open for 0% -> 0% of each run, Pallas kernels for 3% -> 3%
where the time goes in v4:
time: 63.8 us; the launch traced here: 63.4 us
  starting transfers between devices  41 us (64%)
  Pallas kernels  10.8 us (17%)
  waiting for transfers between devices  10.8 us (17%)
  between operations  0.74 us (1%)
    all_to_all x1, starting transfers between devices, body(): lax.all_to_all(out_1, 'azim', split_axis=0, concat_axis=0, tiled=True)  17.6 us
    ppermute x1, starting transfers between devices, swaps(): return (lax.ppermute(far, axis, odd), near)  11 us
    all_to_all x1, waiting for transfers between devices, body(): lax.all_to_all(out_2, 'azim', split_axis=0, concat_axis=0, tiled=True)  9.22 us
    all_to_all x1, starting transfers between devices, body(): lax.all_to_all(out_2, 'azim', split_axis=0, concat_axis=0, tiled=True)  8.57 us
    pallas_call x1, Pallas kernels, body(): kernel(lambda *refs: middle_kernel(aspect, *refs), [planes, (block, F32),...  3.93 us
    pallas_call x1, Pallas kernels, body(): kernel(first_kernel, [(block, F32), ((3, n1, LANES), F32)], [pltpu.VMEM((...  3.17 us
    ppermute x2, starting transfers between devices, shifts(): return (lax.ppermute(first, axis, ahead), lax.ppermute(last, axis, behind))  1.92 us
    ppermute x1, starting transfers between devices, swaps(): near = lax.ppermute(near, axis, even)  1.92 us
  transfers between devices with their start and end apart: 6, of which 3 were waited for; matrix products, arithmetic and copies ran while one was open for 0% of the time, Pallas kernels for 3%

profile of v4, /device:TPU:1, one launch (start us, length us, event | category | flops | bytes accessed | tf_op | source)
XLA Modules:
  0.0 63.4 jit_solution(1753414267104331890)
XLA Ops:
  0.6 3.2 %shard_map.95 = (f32[16,24,128]{2,1,0:T(8,128)}, f32[3,16,128]{2,1,0:T(8,128)}) custom-call(f32[3,128,128]{2,1,0:T(8,128)} %bitcast.9, f32[16,128]{1,0:T(8,128)} %bitcast.18, f32[16,128]{1,0:T(8,128)} %bitcast.19, f32[16,128]{1,0:T(8,128)} %bitcast.20, s32[16,128]{1,0:T(8,128)} %bitcast.16, s32[16,128]{1,0:T(8,128)} %bitcast.21), custom_call_target="tpu_custom_call" | custom-call | flops 3000000000 | tf_op jit(solution)/shard_map/pallas_call | solution.py:515
  3.8 0.0 copy-start
  3.8 0.0 copy-start.3
  3.8 0.0 copy-start.4
  3.8 17.6 %all-to-all-start = ((f32[16,24,128]{2,1,0:T(8,128)}), f32[16,24,128]{2,1,0:T(8,128)S(1)}, u32[]{:S(2)}, u32[]{:S(2)}) async-start(f32[16,24,128]{2,1,0:T(8,128)} %get-tuple-element.20), calls=%async_computation | async-start | bytes 393216 | tf_op jit(solution)/shard_map/all_to_all | solution.py:535
  21.5 0.0 copy-done
  21.5 0.0 copy-done.3
  21.5 0.0 copy-done.4
  21.5 0.0 copy-start.1
  21.5 0.7 %shard_map.96 = (f32[3,128,128]{2,1,0:T(8,128)S(1)}, f32[9,8,128]{2,1,0:T(8,128)S(1)}, f32[9,8,128]{2,1,0:T(8,128)S(1)}, f32[9,16,128]{2,1,0:T(8,128)S(1)}, f32[9,16,128]{2,1,0:T(8,128)S(1)}) custom-call(f32[3,16,128]{2,1,0:T(8,128)S(1)} %copy-done.4, s32[16,128]{1,0:T(8,128)S(1)} %bitcast.17, f32[3,128,128]{2,1,0:T(8,128)S(1)} %bitcast.10), custom_call_target="tpu_custom_call" | custom-call | flops 1400000000 | tf_op jit(solution)/shard_map/pallas_call | solution.py:536
  22.2 11.0 %collective-permute-start = (f32[9,8,128]{2,1,0:T(8,128)S(1)}, f32[9,8,128]{2,1,0:T(8,128)S(1)}, u32[]{:S(2)}, u32[]{:S(2)}) collective-permute-start(f32[9,8,128]{2,1,0:T(8,128)S(1)} %get-tuple-element.16), channel_id=1, source_target_pairs={{0,1008},{16,32},{32,16},{48,64},{64,48},{80,96},{96,80},{112,128}... | collective-permute-start | bytes 110600 | tf_op jit(solution)/shard_map/ppermute | solution.py:497
  33.2 1.9 %collective-permute-start.1 = (f32[9,8,128]{2,1,0:T(8,128)S(1)}, f32[9,8,128]{2,1,0:T(8,128)S(1)}, u32[]{:S(2)}, u32[]{:S(2)}) collective-permute-start(f32[9,8,128]{2,1,0:T(8,128)S(1)} %get-tuple-element.17), channel_id=1, source_target_pairs={{0,16},{16,0},{32,48},{48,32},{64,80},{80,64},{96,112},{112,96},{1... | collective-permute-start | bytes 110600 | tf_op jit(solution)/shard_map/ppermute | solution.py:496
  35.1 0.4 collective-permute-start.2
  35.5 1.5 %collective-permute-start.3 = (f32[9,16,128]{2,1,0:T(8,128)S(1)}, f32[9,16,128]{2,1,0:T(8,128)S(1)}, u32[]{:S(2)}, u32[]{:S(2)}) collective-permute-start(f32[9,16,128]{2,1,0:T(8,128)S(1)} %get-tuple-element.19), channel_id=1, source_target_pairs={{0,1},{1,2},{2,3},{3,4},{4,5},{5,6},{6,7},{7,8},{8,9},{9,10},{10,1... | collective-permute-start | bytes 221192 | tf_op jit(solution)/shard_map/ppermute | solution.py:489
  37.0 0.0 copy-done.1
  37.0 0.0 copy-start.2
  37.0 0.4 shard_map.97.refs_8_
  37.4 0.0 collective-permute-done.refs_2_.refs_3_
  37.4 0.5 collective-permute-done.1.refs_3_.refs_4_
  37.9 1.2 %collective-permute-done.2.refs_4_.refs_5_ = f32[9,16,128]{2,1,0:T(8,128)S(1)} collective-permute-done((f32[9,16,128]{2,1,0:T(8,128)S(1)}, f32[9,16,128]{2,1,0:T(8,128)S(1)}, u32[]{:S(2)}, u32[]{:S(2)}) %collective-permute-start.2) | collective-permute-done | bytes 73760 | tf_op jit(solution)/shard_map/ppermute | solution.py:489
  39.1 0.0 collective-permute-done.3.refs_5_.refs_6_
  39.1 0.0 all-to-all-done.refs_6_.refs_7_
  39.1 0.0 copy-done.2
  39.1 3.9 %shard_map.98 = (f32[3,128,128]{2,1,0:T(8,128)S(1)}, f32[16,24,128]{2,1,0:T(8,128)}, f32[3,32,128]{2,1,0:T(8,128)S(1)}) custom-call(f32[3,128,128]{2,1,0:T(8,128)S(1)} %bitcast.11, f32[3,128,128]{2,1,0:T(8,128)S(1)} %get-tuple-element.15.refs_1_, f32[9,8,128]{2,1,0:T(8,128)S(1)} %collective-permute-done.refs_2_.refs_3_, ...), custom_call_target="tpu_custom_call" | custom-call | flops 4000000000 | tf_op jit(solution)/shard_map/pallas_call | solution.py:548
  43.0 8.6 %all-to-all-start.1 = ((f32[16,24,128]{2,1,0:T(8,128)}), f32[16,24,128]{2,1,0:T(8,128)S(1)}, u32[]{:S(2)}, u32[]{:S(2)}) async-start(f32[16,24,128]{2,1,0:T(8,128)} %get-tuple-element.23), calls=%async_computation.1 | async-start | bytes 393216 | tf_op jit(solution)/shard_map/all_to_all | solution.py:555
  51.6 1.1 %shard_map.99.refs_2_ = f32[3,128,128]{2,1,0:T(8,128)S(1)} custom-call(f32[3,32,128]{2,1,0:T(8,128)S(1)} %get-tuple-element.22.source, s32[32,128]{1,0:T(8,128)S(1)} %bitcast.15), custom_call_target="tpu_custom_call" | custom-call | flops 1000000000 | tf_op jit(solution)/shard_map/pallas_call | solution.py:556
  52.7 9.2 %all-to-all-done.1.refs_8_ = f32[16,24,128]{2,1,0:T(8,128)S(1)} async-done(((f32[16,24,128]{2,1,0:T(8,128)}), f32[16,24,128]{2,1,0:T(8,128)S(1)}, u32[]{:S(2)}, u32[]{:S(2)}) %all-to-all-start.1) | async-done | bytes 196640 | tf_op jit(solution)/shard_map/all_to_all | solution.py:555
  61.9 1.5 %shard_map.100 = (f32[3,128,128]{2,1,0:T(8,128)}, f32[6,4096]{1,0:T(8,128)}) custom-call(f32[3,128,128]{2,1,0:T(8,128)S(1)} %bitcast.12, f32[3,128,128]{2,1,0:T(8,128)S(1)} %get-tuple-element.21.refs_1_, f32[3,128,128]{2,1,0:T(8,128)S(1)} %shard_map.99.refs_2_, f32[9,8,128]{2,1,0:T(8,128)S(1)} %collective-permute-done.refs_2_.refs_3_, ...), custom_call_target="tpu_custom_call" | custom-call | flops 1800000000 | tf_op jit(solution)/shard_map/pallas_call | solution.py:557
Async XLA Ops:
  3.8 17.6 %copy-start = (f32[3,16,8,128]{3,2,1,0:T(8,128)S(1)}, f32[3,16,8,128]{3,2,1,0:T(8,128)}, u32[]{:S(2)}) copy-start(f32[3,16,8,128]{3,2,1,0:T(8,128)} %param.8) | copy-start | bytes 589828
  3.8 17.6 %copy-start.3 = (s32[2048]{0:T(1024)S(1)}, s32[2048]{0:T(1024)}, u32[]{:S(2)}) copy-start(s32[2048]{0:T(1024)} %param.13) | copy-start | bytes 24580
  3.8 17.6 %copy-start.4 = (f32[3,16,128]{2,1,0:T(8,128)S(1)}, f32[3,16,128]{2,1,0:T(8,128)}, u32[]{:S(2)}) copy-start(f32[3,16,128]{2,1,0:T(8,128)} %get-tuple-element.14.refs_0_) | copy-start | bytes 73732
  3.8 35.2 %all-to-all-start = ((f32[16,24,128]{2,1,0:T(8,128)}), f32[16,24,128]{2,1,0:T(8,128)S(1)}, u32[]{:S(2)}, u32[]{:S(2)}) async-start(f32[16,24,128]{2,1,0:T(8,128)} %get-tuple-element.20), calls=%async_computation | async-start | bytes 393216 | tf_op jit(solution)/shard_map/all_to_all | solution.py:535
  21.5 15.6 %copy-start.1 = (s32[4096,1]{0,1:T(1,128)S(1)}, s32[4096,1]{0,1:T(1,128)}, u32[]{:S(2)}) copy-start(s32[4096,1]{0,1:T(1,128)} %param.14) | copy-start | bytes 49156
  22.2 15.2 %collective-permute-start = (f32[9,8,128]{2,1,0:T(8,128)S(1)}, f32[9,8,128]{2,1,0:T(8,128)S(1)}, u32[]{:S(2)}, u32[]{:S(2)}) collective-permute-start(f32[9,8,128]{2,1,0:T(8,128)S(1)} %get-tuple-element.16), channel_id=1, source_target_pairs={{0,1008},{16,32},{32,16},{48,64},{64,48},{80,96},{96,80},{112,128}... | collective-permute-start | bytes 110600 | tf_op jit(solution)/shard_map/ppermute | solution.py:497
  33.2 4.7 %collective-permute-start.1 = (f32[9,8,128]{2,1,0:T(8,128)S(1)}, f32[9,8,128]{2,1,0:T(8,128)S(1)}, u32[]{:S(2)}, u32[]{:S(2)}) collective-permute-start(f32[9,8,128]{2,1,0:T(8,128)S(1)} %get-tuple-element.17), channel_id=1, source_target_pairs={{0,16},{16,0},{32,48},{48,32},{64,80},{80,64},{96,112},{112,96},{1... | collective-permute-start | bytes 110600 | tf_op jit(solution)/shard_map/ppermute | solution.py:496
  35.1 3.9 %collective-permute-start.2 = (f32[9,16,128]{2,1,0:T(8,128)S(1)}, f32[9,16,128]{2,1,0:T(8,128)S(1)}, u32[]{:S(2)}, u32[]{:S(2)}) collective-permute-start(f32[9,16,128]{2,1,0:T(8,128)S(1)} %get-tuple-element.18), channel_id=1, source_target_pairs={{1,0},{2,1},{3,2},{4,3},{5,4},{6,5},{7,6},{8,7},{9,8},{10,9},{11,1... | collective-permute-start | bytes 221192 | tf_op jit(solution)/shard_map/ppermute | solution.py:489
  35.5 3.6 %collective-permute-start.3 = (f32[9,16,128]{2,1,0:T(8,128)S(1)}, f32[9,16,128]{2,1,0:T(8,128)S(1)}, u32[]{:S(2)}, u32[]{:S(2)}) collective-permute-start(f32[9,16,128]{2,1,0:T(8,128)S(1)} %get-tuple-element.19), channel_id=1, source_target_pairs={{0,1},{1,2},{2,3},{3,4},{4,5},{5,6},{6,7},{7,8},{8,9},{9,10},{10,1... | collective-permute-start | bytes 221192 | tf_op jit(solution)/shard_map/ppermute | solution.py:489
  37.0 2.0 %copy-start.2 = (s32[4096]{0:T(1024)S(1)}, s32[4096]{0:T(1024)}, u32[]{:S(2)}) copy-start(s32[4096]{0:T(1024)} %param.15) | copy-start | bytes 49156
  43.0 18.9 %all-to-all-start.1 = ((f32[16,24,128]{2,1,0:T(8,128)}), f32[16,24,128]{2,1,0:T(8,128)S(1)}, u32[]{:S(2)}, u32[]{:S(2)}) async-start(f32[16,24,128]{2,1,0:T(8,128)} %get-tuple-element.23), calls=%async_computation.1 | async-start | bytes 393216 | tf_op jit(solution)/shard_map/all_to_all | solution.py:555
